TPU v7x, 128 devices: a whole 4x4x4 slice. The times are simulated.
128 devices in a mesh: row: 16 (over x, z), col: 8 (over y, core).
Axes of the slice: x: 4, y: 4, z: 4, core: 2. Of those that a mesh axis runs over, the one named last changes fastest.
Arguments:
- sources: float32 [3, 8192, 2048], P(None, 'row', 'col'), may hold values from -1.5 to 1.5
- edge_codes: int32 [2, 8192, 2048], P(None, 'row', 'col'), may hold values from 0 to 15
- seam_labels: int32 [8192, 2048], P('row', 'col'), may hold values from 0 to 4, as said below
Outputs:
- solution: float32 [3, 8192, 2048], P(None, 'row', 'col')
- residual: float32 [3, 8192, 2048], P(None, 'row', 'col')
Inputs may be any that keep to these rules, and one draw needn't show every extreme that they name: `seam_labels`: label of the source image from which each pixel was taken.
All inputs are finite; a program needn't handle non-finite values.
Results may differ from a plain program's by a relative error of at most 0.00085.
Values sent between devices are 32-bit elements; how exact they have to be, the bound alone decides.
A program may use at most 192 MiB of HBM per device.

v0:
```python
import math

import jax
import jax.numpy as jnp
from jax import lax
from jax.sharding import PartitionSpec as P

SWEEPS = 4
CYCLES = 2


screen = 2e-05
seam_factor = 0.2
coarse_scale = 0.0625


def padded_2(value, sides, width):
    for axis, dim in sides:
        devices, length = (lax.axis_size(axis), value.shape[dim])
        up = [(i, (i + 1) % devices) for i in range(devices - 1)]
        down = [(j, i) for i, j in up]
        last = lax.slice_in_dim(value, length - width, length, axis=dim)
        first = lax.slice_in_dim(value, 0, width, axis=dim)
        before = lax.ppermute(last, axis, up)
        after = lax.ppermute(first, axis, down)
        value = jnp.concatenate([before, value, after], axis=dim)
    return value


def chebyshev_weight(sweep_index):
    return 1.0 / (1.25 + 0.75 * math.cos(math.pi * (2 * sweep_index + 1) / (2 * SWEEPS)))


def edge_weight(code, left_label, right_label):
    strength = jnp.exp2(code.astype(jnp.float32) * 0.25 - 2.0)
    return strength * jnp.where(left_label != right_label, seam_factor, 1.0).astype(jnp.float32)


def coarsen_faces(face_x, face_y):
    picked_x = face_x[:, ::4]
    new_x = picked_x.reshape(picked_x.shape[0] // 4, 4, picked_x.shape[1]).sum(axis=1) / 16.0
    picked_y = face_y[::4, :]
    new_y = picked_y.reshape(picked_y.shape[0], picked_y.shape[1] // 4, 4).sum(axis=2) / 16.0
    return (new_x, new_y)


def cell_weights(face_x, face_y):
    weights = jnp.stack([face_x[:, :-1], face_x[:, 1:], face_y[:-1, :], face_y[1:, :]])
    diagonal = screen + weights[0] + weights[1] + weights[2] + weights[3]
    return (weights, diagonal)


def apply_cells(padded, weights, diagonal):
    centre = padded[:, 1:-1, 1:-1]
    result = (
        diagonal * centre - weights[0] * padded[:, 1:-1, :-2] - weights[1] * padded[:, 1:-1, 2:]
    )
    return result - weights[2] * padded[:, :-2, 1:-1] - weights[3] * padded[:, 2:, 1:-1]


def block_mean(current):
    shape = current.shape
    return current.reshape(shape[0], shape[1] // 4, 4, shape[2] // 4, 4).mean(axis=(2, 4))


def expand(current):
    return jnp.repeat(jnp.repeat(current, 4, axis=1), 4, axis=2)


def sine_table(first, count, extent):
    rows_idx = first + jnp.arange(count, dtype=jnp.int32) + 1
    cols_idx = jnp.arange(extent, dtype=jnp.int32) + 1
    product = rows_idx[:, None] * cols_idx[None, :] % (2 * (extent + 1))
    return math.sqrt(2.0 / (extent + 1)) * jnp.sin(
        jnp.pi * product.astype(jnp.float32) / (extent + 1)
    )


def eigen_values(row_count, row_extent, col_count, col_extent):
    row_modes = (jnp.arange(row_count, dtype=jnp.int32) + 1).astype(jnp.float32)
    col_modes = (jnp.arange(col_count, dtype=jnp.int32) + 1).astype(jnp.float32)
    row_part = 2.0 - 2.0 * jnp.cos(jnp.pi * row_modes / (row_extent + 1))
    col_part = 2.0 - 2.0 * jnp.cos(jnp.pi * col_modes / (col_extent + 1))
    return screen + coarse_scale * (row_part[:, None] + col_part[None, :])


def local(sources, edge_codes, seam_labels):
    rows_here, cols_here = (sources.shape[1], sources.shape[2])
    row_devices = lax.axis_size("row")
    col_devices = lax.axis_size("col")
    row_position = lax.axis_index("row")
    col_position = lax.axis_index("col")
    img_rows = rows_here * row_devices
    img_cols = cols_here * col_devices
    highest = lax.Precision.HIGHEST
    stacked = jnp.concatenate([edge_codes, seam_labels[None]], axis=0)
    beside_all = padded_2(stacked, (("row", 1), ("col", 2)), 1)
    left_cols = col_position * cols_here + jnp.arange(cols_here + 1, dtype=jnp.int32) - 1
    upper_rows = row_position * rows_here + jnp.arange(rows_here + 1, dtype=jnp.int32) - 1
    inner_x = edge_weight(
        beside_all[0, 1:-1, 0 : cols_here + 1],
        beside_all[2, 1:-1, 0 : cols_here + 1],
        beside_all[2, 1:-1, 1 : cols_here + 2],
    )
    inner_y = edge_weight(
        beside_all[1, 0 : rows_here + 1, 1:-1],
        beside_all[2, 0 : rows_here + 1, 1:-1],
        beside_all[2, 1 : rows_here + 2, 1:-1],
    )
    face_x = jnp.where(((left_cols >= 0) & (left_cols <= img_cols - 2))[None, :], inner_x, 1.0)
    face_y = jnp.where(((upper_rows >= 0) & (upper_rows <= img_rows - 2))[:, None], inner_y, 1.0)
    fine_w, fine_diag = cell_weights(face_x, face_y)
    level_x, level_y = coarsen_faces(face_x, face_y)
    level_w, level_diag = cell_weights(level_x, level_y)

    def fine_apply(current):
        padded = padded_2(current, (("row", 1), ("col", 2)), 1)
        return apply_cells(padded, fine_w, fine_diag)

    def fine_smooth(current, from_zero):
        for sweep_index in range(SWEEPS):
            omega = chebyshev_weight(sweep_index)
            if sweep_index == 0 and from_zero:
                current = omega * sources / fine_diag
            else:
                current = current + omega * (sources - fine_apply(current)) / fine_diag
        return current

    def level_apply(current):
        padded = padded_2(current, (("row", 1), ("col", 2)), 1)
        return apply_cells(padded, level_w, level_diag)

    def level_smooth(current, source, from_zero):
        for sweep_index in range(SWEEPS):
            omega = chebyshev_weight(sweep_index)
            if sweep_index == 0 and from_zero:
                current = omega * source / level_diag
            else:
                current = current + omega * (source - level_apply(current)) / level_diag
        return current

    coarse_rows_here = rows_here // 16
    coarse_cols_here = cols_here // 16
    count_rows = coarse_rows_here * row_devices
    count_cols = coarse_cols_here * col_devices
    table_cols = sine_table(0, count_cols, count_cols)
    table_rows = sine_table(0, count_rows, count_rows)
    own_cols = sine_table(col_position * coarse_cols_here, coarse_cols_here, count_cols)
    solution = jnp.zeros_like(sources)
    for cycle_index in range(CYCLES):
        solution = fine_smooth(solution, cycle_index == 0)
        fine_res = sources - fine_apply(solution)
        level_src = block_mean(fine_res)
        level_field = level_smooth(jnp.zeros_like(level_src), level_src, True)
        level_res = level_src - level_apply(level_field)
        partial_value = jnp.einsum(
            "cij,jl->cil",
            lax.all_gather(block_mean(level_res), "col", axis=2, tiled=True),
            table_cols,
            precision=highest,
        )
        spectrum = jnp.einsum(
            "ki,cij->ckj",
            table_rows,
            lax.all_gather(partial_value, "row", axis=1, tiled=True),
            precision=highest,
        )
        scaled = spectrum / eigen_values(count_rows, count_rows, count_cols, count_cols)
        own_rows = sine_table(row_position * coarse_rows_here, coarse_rows_here, count_rows)
        back = jnp.einsum("ki,cij->ckj", own_rows, scaled, precision=highest)
        correction = jnp.einsum("cij,lj->cil", back, own_cols, precision=highest)
        level_field = level_smooth(level_field + expand(correction), level_src, False)
        solution = fine_smooth(solution + expand(level_field), False)
    residual = sources - fine_apply(solution)
    return (solution, residual)


def solution(mesh):
    in_specs = (P(None, "row", "col"), P(None, "row", "col"), P("row", "col"))
    out_specs = (P(None, "row", "col"), P(None, "row", "col"))
    return jax.shard_map(local, mesh=mesh, in_specs=in_specs, out_specs=out_specs, check_vma=False)
```

profile of v0, /device:TPU:1, one launch (start us, length us, event | category | flops | bytes accessed | tf_op | source)
XLA Modules:
  0.0 1139.3 jit_solution(15540146213797442810)
XLA Ops:
  4.6 5.8 collective-permute-start
  12.3 4.4 collective-permute-done.1
  34.8 7.4 collective-permute-done.4
  57.9 4.6 collective-permute-start.8
  63.9 6.2 collective-permute-done.8
  70.0 6.7 collective-permute-done.9
  90.5 5.5 collective-permute-start.12
  97.3 7.4 slice.1067
  121.5 5.7 fusion.176
  127.4 4.7 collective-permute-start.16
  133.4 7.5 collective-permute-done.16
  158.3 54.1 %reshape.163 = f32[3,128,4,64,4]{4,3,2,1,0:T(8,128)} reshape(f32[3,512,256]{2,1,0:T(8,128)} %copy.158) | data formatting | bytes 3145728 | tf_op jit(solution)/shard_map/reshape | solution.py:63
  212.4 17.8 %reduce_sum.54 = f32[3,128,64]{2,1,0:T(8,128)S(1)} reduce(f32[3,128,4,64,4]{4,3,2,1,0:T(8,128)} %reshape.163, f32[]{:T(128)} %constant.70.clone.1), dimensions={2,4}, to_apply=%region_0.1 | reduce | flops 368640 | bytes 1671172 | tf_op jit(solution)/shard_map/reduce_sum | solution.py:63
  249.3 5.5 collective-permute-start.24
  285.0 4.4 collective-permute-done.31
  316.1 5.1 reshape.166
  324.7 10.5 all_gather.12
  335.8 22.5 %all_gather.13 = f32[3,512,128]{2,1,0:T(8,128)S(1)} all-gather(f32[3,32,128]{2,1,0:T(8,128)S(1)} %fusion.450), channel_id=1, replica_groups=mesh['row'=16,'col'=8] {'row'}, dimensions={1}, use_global_device_ids=true | all-gather | bytes 835584 | tf_op jit(solution)/shard_map/all_gather | solution.py:165
  358.3 7.5 fusion.208
  379.6 9.4 collective-permute-start.38
  414.2 5.4 collective-permute-start.44
  448.9 4.4 collective-permute-done.51
  478.0 5.5 collective-permute-start.54
  496.3 6.2 collective-permute-done.56
  522.3 6.2 collective-permute-done.60
  549.7 6.2 collective-permute-done.64
  576.4 6.2 collective-permute-done.68
  602.2 6.2 collective-permute-done.72
  627.2 6.6 collective-permute-done.76
  652.6 6.6 collective-permute-done.80
  678.1 6.6 collective-permute-done.84
  701.9 54.1 %reshape.171 = f32[3,128,4,64,4]{4,3,2,1,0:T(8,128)} reshape(f32[3,512,256]{2,1,0:T(8,128)} %copy.176) | data formatting | bytes 3145728 | tf_op jit(solution)/shard_map/reshape | solution.py:63
  756.0 17.8 %reduce_sum.58 = f32[3,128,64]{2,1,0:T(8,128)S(1)} reduce(f32[3,128,4,64,4]{4,3,2,1,0:T(8,128)} %reshape.171, f32[]{:T(128)} %constant.70.clone.1), dimensions={2,4}, to_apply=%region_4.5 | reduce | flops 368640 | bytes 1671172 | tf_op jit(solution)/shard_map/reduce_sum | solution.py:63
  788.2 4.4 collective-permute-done.91
  825.8 4.4 collective-permute-done.99
  851.7 5.1 reshape.172
  860.3 9.9 all_gather.14
  870.8 21.0 %all_gather.15 = f32[3,512,128]{2,1,0:T(8,128)S(1)} all-gather(f32[3,32,128]{2,1,0:T(8,128)S(1)} %fusion.448), channel_id=1, replica_groups=mesh['row'=16,'col'=8] {'row'}, dimensions={1}, use_global_device_ids=true | all-gather | bytes 835584 | tf_op jit(solution)/shard_map/all_gather | solution.py:165
  891.7 7.5 fusion.207
  914.7 9.6 collective-permute-start.106
  945.0 4.4 collective-permute-done.111
  949.6 5.7 collective-permute-start.112
  1012.0 5.5 collective-permute-start.122
  1030.3 6.2 collective-permute-done.124
  1056.3 6.2 collective-permute-done.128
  1083.7 6.2 collective-permute-done.132
  1110.4 6.2 collective-permute-done.136
  1129.4 6.5 fusion.2
  (492 shorter events, 686.6 us)
Async XLA Ops:
  3.3 13.4 %collective-permute-start.1 = (s32[3,1,256]{1,2,0:T(8,128)}, s32[3,1,256]{1,2,0:T(8,128)S(1)}, u32[]{:S(2)}, u32[]{:S(2)}) collective-permute-start(s32[3,1,256]{1,2,0:T(8,128)} %get-tuple-element.86), channel_id=1, source_target_pairs={{8,0},{16,8},{24,16},{32,24},{40,32},{48,40},{56,48},{64,56},{72,6... | collective-permute-start | bytes 9224 | tf_op jit(solution)/shard_map/ppermute | solution.py:25
  4.6 13.1 %collective-permute-start = (s32[3,1,256]{1,2,0:T(8,128)}, s32[3,1,256]{1,2,0:T(8,128)}, u32[]{:S(2)}, u32[]{:S(2)}) collective-permute-start(s32[3,1,256]{1,2,0:T(8,128)} %get-tuple-element.87), channel_id=1, source_target_pairs={{0,8},{8,16},{16,24},{24,32},{32,40},{40,48},{48,56},{56,64},{64,7... | collective-permute-start | bytes 9224 | tf_op jit(solution)/shard_map/ppermute | solution.py:24
  18.6 8.0 collective-permute-start.3
  29.4 12.8 %collective-permute-start.4 = (f32[3,1,256]{1,2,0:T(8,128)S(1)}, f32[3,1,256]{1,2,0:T(8,128)S(1)}, u32[]{:S(2)}, u32[]{:S(2)}) collective-permute-start(f32[3,1,256]{1,2,0:T(8,128)S(1)} %get-tuple-element.84), channel_id=1, source_target_pairs={{0,8},{8,16},{16,24},{24,32},{32,40},{40,48},{48,56},{56,64},{64,7... | collective-permute-start | bytes 9224 | tf_op jit(solution)/shard_map/ppermute | solution.py:24
  33.5 13.0 %collective-permute-start.5 = (f32[3,1,256]{1,2,0:T(8,128)S(1)}, f32[3,1,256]{1,2,0:T(8,128)S(1)}, u32[]{:S(2)}, u32[]{:S(2)}) collective-permute-start(f32[3,1,256]{1,2,0:T(8,128)S(1)} %get-tuple-element.85), channel_id=1, source_target_pairs={{8,0},{16,8},{24,16},{32,24},{40,32},{48,40},{56,48},{64,56},{72,6... | collective-permute-start | bytes 9224 | tf_op jit(solution)/shard_map/ppermute | solution.py:25
  57.9 12.1 %collective-permute-start.8 = (f32[3,1,256]{1,2,0:T(8,128)S(1)}, f32[3,1,256]{1,2,0:T(8,128)S(1)}, u32[]{:S(2)}, u32[]{:S(2)}) collective-permute-start(f32[3,1,256]{1,2,0:T(8,128)S(1)} %get-tuple-element.82), channel_id=1, source_target_pairs={{0,8},{8,16},{16,24},{24,32},{32,40},{40,48},{48,56},{56,64},{64,7... | collective-permute-start | bytes 9224 | tf_op jit(solution)/shard_map/ppermute | solution.py:24
  62.6 14.1 %collective-permute-start.9 = (f32[3,1,256]{1,2,0:T(8,128)S(1)}, f32[3,1,256]{1,2,0:T(8,128)S(1)}, u32[]{:S(2)}, u32[]{:S(2)}) collective-permute-start(f32[3,1,256]{1,2,0:T(8,128)S(1)} %get-tuple-element.83), channel_id=1, source_target_pairs={{8,0},{16,8},{24,16},{32,24},{40,32},{48,40},{56,48},{64,56},{72,6... | collective-permute-start | bytes 9224 | tf_op jit(solution)/shard_map/ppermute | solution.py:25
  90.5 19.2 %collective-permute-start.12 = (f32[3,1,256]{1,2,0:T(8,128)}, f32[3,1,256]{1,2,0:T(8,128)S(1)}, u32[]{:S(2)}, u32[]{:S(2)}) collective-permute-start(f32[3,1,256]{1,2,0:T(8,128)} %get-tuple-element.80), channel_id=1, source_target_pairs={{0,8},{8,16},{16,24},{24,32},{32,40},{40,48},{48,56},{56,64},{64,7... | collective-permute-start | bytes 9224 | tf_op jit(solution)/shard_map/ppermute | solution.py:24
  96.0 13.7 %collective-permute-start.13 = (f32[3,1,256]{1,2,0:T(8,128)}, f32[3,1,256]{1,2,0:T(8,128)}, u32[]{:S(2)}, u32[]{:S(2)}) collective-permute-start(f32[3,1,256]{1,2,0:T(8,128)} %get-tuple-element.81), channel_id=1, source_target_pairs={{8,0},{16,8},{24,16},{32,24},{40,32},{48,40},{56,48},{64,56},{72,6... | collective-permute-start | bytes 9224 | tf_op jit(solution)/shard_map/ppermute | solution.py:25
  110.7 10.7 collective-permute-start.14
  113.0 8.5 collective-permute-start.15
  127.4 13.5 %collective-permute-start.16 = (f32[3,1,256]{1,2,0:T(8,128)S(1)}, f32[3,1,256]{1,2,0:T(8,128)S(1)}, u32[]{:S(2)}, u32[]{:S(2)}) collective-permute-start(f32[3,1,256]{1,2,0:T(8,128)S(1)} %get-tuple-element.78), channel_id=1, source_target_pairs={{0,8},{8,16},{16,24},{24,32},{32,40},{40,48},{48,56},{56,64},{64,7... | collective-permute-start | bytes 9224 | tf_op jit(solution)/shard_map/ppermute | solution.py:24
  132.1 13.1 %collective-permute-start.17 = (f32[3,1,256]{1,2,0:T(8,128)S(1)}, f32[3,1,256]{1,2,0:T(8,128)S(1)}, u32[]{:S(2)}, u32[]{:S(2)}) collective-permute-start(f32[3,1,256]{1,2,0:T(8,128)S(1)} %get-tuple-element.79), channel_id=1, source_target_pairs={{8,0},{16,8},{24,16},{32,24},{40,32},{48,40},{56,48},{64,56},{72,6... | collective-permute-start | bytes 9224 | tf_op jit(solution)/shard_map/ppermute | solution.py:25
  282.0 7.4 collective-permute-start.31
  379.6 12.1 %collective-permute-start.38 = (f32[3,130,1]{2,1,0:T(8,128)S(1)}, f32[3,130,1]{2,1,0:T(8,128)S(1)}, u32[]{:S(2)}, u32[]{:S(2)}) collective-permute-start(f32[3,130,1]{2,1,0:T(8,128)S(1)} %get-tuple-element.115), channel_id=1, source_target_pairs={{0,1},{1,2},{2,3},{3,4},{4,5},{5,6},{6,7},{8,9},{9,10},{10,11},{11... | collective-permute-start | bytes 4688 | tf_op jit(solution)/shard_map/ppermute | solution.py:24
  446.1 7.1 collective-permute-start.51
  464.3 9.5 collective-permute-start.52
  468.2 9.7 collective-permute-start.53
  478.0 7.5 collective-permute-start.54
  491.2 11.2 collective-permute-start.56
  495.0 11.6 %collective-permute-start.57 = (f32[3,1,256]{1,2,0:T(8,128)S(1)}, f32[3,1,256]{1,2,0:T(8,128)S(1)}, u32[]{:S(2)}, u32[]{:S(2)}) collective-permute-start(f32[3,1,256]{1,2,0:T(8,128)S(1)} %get-tuple-element.75), channel_id=1, source_target_pairs={{8,0},{16,8},{24,16},{32,24},{40,32},{48,40},{56,48},{64,56},{72,6... | collective-permute-start | bytes 9224 | tf_op jit(solution)/shard_map/ppermute | solution.py:25
  517.0 11.5 %collective-permute-start.60 = (f32[3,1,256]{1,2,0:T(8,128)S(1)}, f32[3,1,256]{1,2,0:T(8,128)S(1)}, u32[]{:S(2)}, u32[]{:S(2)}) collective-permute-start(f32[3,1,256]{1,2,0:T(8,128)S(1)} %get-tuple-element.72), channel_id=1, source_target_pairs={{0,8},{8,16},{16,24},{24,32},{32,40},{40,48},{48,56},{56,64},{64,7... | collective-permute-start | bytes 9224 | tf_op jit(solution)/shard_map/ppermute | solution.py:24
  521.0 11.6 %collective-permute-start.61 = (f32[3,1,256]{1,2,0:T(8,128)S(1)}, f32[3,1,256]{1,2,0:T(8,128)S(1)}, u32[]{:S(2)}, u32[]{:S(2)}) collective-permute-start(f32[3,1,256]{1,2,0:T(8,128)S(1)} %get-tuple-element.73), channel_id=1, source_target_pairs={{8,0},{16,8},{24,16},{32,24},{40,32},{48,40},{56,48},{64,56},{72,6... | collective-permute-start | bytes 9224 | tf_op jit(solution)/shard_map/ppermute | solution.py:25
  544.7 11.2 collective-permute-start.64
  548.4 11.6 %collective-permute-start.65 = (f32[3,1,256]{1,2,0:T(8,128)S(1)}, f32[3,1,256]{1,2,0:T(8,128)S(1)}, u32[]{:S(2)}, u32[]{:S(2)}) collective-permute-start(f32[3,1,256]{1,2,0:T(8,128)S(1)} %get-tuple-element.71), channel_id=1, source_target_pairs={{8,0},{16,8},{24,16},{32,24},{40,32},{48,40},{56,48},{64,56},{72,6... | collective-permute-start | bytes 9224 | tf_op jit(solution)/shard_map/ppermute | solution.py:25
  571.1 11.5 %collective-permute-start.68 = (f32[3,1,256]{1,2,0:T(8,128)S(1)}, f32[3,1,256]{1,2,0:T(8,128)S(1)}, u32[]{:S(2)}, u32[]{:S(2)}) collective-permute-start(f32[3,1,256]{1,2,0:T(8,128)S(1)} %get-tuple-element.68), channel_id=1, source_target_pairs={{0,8},{8,16},{16,24},{24,32},{32,40},{40,48},{48,56},{56,64},{64,7... | collective-permute-start | bytes 9224 | tf_op jit(solution)/shard_map/ppermute | solution.py:24
  575.1 11.6 %collective-permute-start.69 = (f32[3,1,256]{1,2,0:T(8,128)S(1)}, f32[3,1,256]{1,2,0:T(8,128)S(1)}, u32[]{:S(2)}, u32[]{:S(2)}) collective-permute-start(f32[3,1,256]{1,2,0:T(8,128)S(1)} %get-tuple-element.69), channel_id=1, source_target_pairs={{8,0},{16,8},{24,16},{32,24},{40,32},{48,40},{56,48},{64,56},{72,6... | collective-permute-start | bytes 9224 | tf_op jit(solution)/shard_map/ppermute | solution.py:25
  596.9 11.5 %collective-permute-start.72 = (f32[3,1,256]{1,2,0:T(8,128)S(1)}, f32[3,1,256]{1,2,0:T(8,128)S(1)}, u32[]{:S(2)}, u32[]{:S(2)}) collective-permute-start(f32[3,1,256]{1,2,0:T(8,128)S(1)} %get-tuple-element.66), channel_id=1, source_target_pairs={{0,8},{8,16},{16,24},{24,32},{32,40},{40,48},{48,56},{56,64},{64,7... | collective-permute-start | bytes 9224 | tf_op jit(solution)/shard_map/ppermute | solution.py:24
  600.9 11.6 %collective-permute-start.73 = (f32[3,1,256]{1,2,0:T(8,128)S(1)}, f32[3,1,256]{1,2,0:T(8,128)S(1)}, u32[]{:S(2)}, u32[]{:S(2)}) collective-permute-start(f32[3,1,256]{1,2,0:T(8,128)S(1)} %get-tuple-element.67), channel_id=1, source_target_pairs={{8,0},{16,8},{24,16},{32,24},{40,32},{48,40},{56,48},{64,56},{72,6... | collective-permute-start | bytes 9224 | tf_op jit(solution)/shard_map/ppermute | solution.py:25
  622.1 11.7 %collective-permute-start.76 = (f32[3,1,256]{1,2,0:T(8,128)S(1)}, f32[3,1,256]{1,2,0:T(8,128)S(1)}, u32[]{:S(2)}, u32[]{:S(2)}) collective-permute-start(f32[3,1,256]{1,2,0:T(8,128)S(1)} %get-tuple-element.64), channel_id=1, source_target_pairs={{0,8},{8,16},{16,24},{24,32},{32,40},{40,48},{48,56},{56,64},{64,7... | collective-permute-start | bytes 9224 | tf_op jit(solution)/shard_map/ppermute | solution.py:24
  625.9 12.1 %collective-permute-start.77 = (f32[3,1,256]{1,2,0:T(8,128)S(1)}, f32[3,1,256]{1,2,0:T(8,128)S(1)}, u32[]{:S(2)}, u32[]{:S(2)}) collective-permute-start(f32[3,1,256]{1,2,0:T(8,128)S(1)} %get-tuple-element.65), channel_id=1, source_target_pairs={{8,0},{16,8},{24,16},{32,24},{40,32},{48,40},{56,48},{64,56},{72,6... | collective-permute-start | bytes 9224 | tf_op jit(solution)/shard_map/ppermute | solution.py:25
  647.6 11.7 %collective-permute-start.80 = (f32[3,1,256]{1,2,0:T(8,128)S(1)}, f32[3,1,256]{1,2,0:T(8,128)S(1)}, u32[]{:S(2)}, u32[]{:S(2)}) collective-permute-start(f32[3,1,256]{1,2,0:T(8,128)S(1)} %get-tuple-element.62), channel_id=1, source_target_pairs={{0,8},{8,16},{16,24},{24,32},{32,40},{40,48},{48,56},{56,64},{64,7... | collective-permute-start | bytes 9224 | tf_op jit(solution)/shard_map/ppermute | solution.py:24
  651.3 12.1 %collective-permute-start.81 = (f32[3,1,256]{1,2,0:T(8,128)S(1)}, f32[3,1,256]{1,2,0:T(8,128)S(1)}, u32[]{:S(2)}, u32[]{:S(2)}) collective-permute-start(f32[3,1,256]{1,2,0:T(8,128)S(1)} %get-tuple-element.63), channel_id=1, source_target_pairs={{8,0},{16,8},{24,16},{32,24},{40,32},{48,40},{56,48},{64,56},{72,6... | collective-permute-start | bytes 9224 | tf_op jit(solution)/shard_map/ppermute | solution.py:25
  673.0 11.7 %collective-permute-start.84 = (f32[3,1,256]{1,2,0:T(8,128)S(1)}, f32[3,1,256]{1,2,0:T(8,128)S(1)}, u32[]{:S(2)}, u32[]{:S(2)}) collective-permute-start(f32[3,1,256]{1,2,0:T(8,128)S(1)} %get-tuple-element.60), channel_id=1, source_target_pairs={{0,8},{8,16},{16,24},{24,32},{32,40},{40,48},{48,56},{56,64},{64,7... | collective-permute-start | bytes 9224 | tf_op jit(solution)/shard_map/ppermute | solution.py:24
  676.8 12.1 %collective-permute-start.85 = (f32[3,1,256]{1,2,0:T(8,128)S(1)}, f32[3,1,256]{1,2,0:T(8,128)S(1)}, u32[]{:S(2)}, u32[]{:S(2)}) collective-permute-start(f32[3,1,256]{1,2,0:T(8,128)S(1)} %get-tuple-element.61), channel_id=1, source_target_pairs={{8,0},{16,8},{24,16},{32,24},{40,32},{48,40},{56,48},{64,56},{72,6... | collective-permute-start | bytes 9224 | tf_op jit(solution)/shard_map/ppermute | solution.py:25
  914.7 12.4 %collective-permute-start.106 = (f32[3,130,1]{2,1,0:T(8,128)S(1)}, f32[3,130,1]{2,1,0:T(8,128)S(1)}, u32[]{:S(2)}, u32[]{:S(2)}) collective-permute-start(f32[3,130,1]{2,1,0:T(8,128)S(1)} %get-tuple-element.99), channel_id=1, source_target_pairs={{0,1},{1,2},{2,3},{3,4},{4,5},{5,6},{6,7},{8,9},{9,10},{10,11},{11... | collective-permute-start | bytes 4688 | tf_op jit(solution)/shard_map/ppermute | solution.py:24
  998.3 9.5 collective-permute-start.120
  1002.2 9.7 collective-permute-start.121
  1012.0 7.5 collective-permute-start.122
  1025.2 11.2 collective-permute-start.124
  1029.0 11.6 %collective-permute-start.125 = (f32[3,1,256]{1,2,0:T(8,128)S(1)}, f32[3,1,256]{1,2,0:T(8,128)S(1)}, u32[]{:S(2)}, u32[]{:S(2)}) collective-permute-start(f32[3,1,256]{1,2,0:T(8,128)S(1)} %get-tuple-element.57), channel_id=1, source_target_pairs={{8,0},{16,8},{24,16},{32,24},{40,32},{48,40},{56,48},{64,56},{72,6... | collective-permute-start | bytes 9224 | tf_op jit(solution)/shard_map/ppermute | solution.py:25
  1051.0 11.5 %collective-permute-start.128 = (f32[3,1,256]{1,2,0:T(8,128)S(1)}, f32[3,1,256]{1,2,0:T(8,128)S(1)}, u32[]{:S(2)}, u32[]{:S(2)}) collective-permute-start(f32[3,1,256]{1,2,0:T(8,128)S(1)} %get-tuple-element.54), channel_id=1, source_target_pairs={{0,8},{8,16},{16,24},{24,32},{32,40},{40,48},{48,56},{56,64},{64,7... | collective-permute-start | bytes 9224 | tf_op jit(solution)/shard_map/ppermute | solution.py:24
  1055.0 11.6 %collective-permute-start.129 = (f32[3,1,256]{1,2,0:T(8,128)S(1)}, f32[3,1,256]{1,2,0:T(8,128)S(1)}, u32[]{:S(2)}, u32[]{:S(2)}) collective-permute-start(f32[3,1,256]{1,2,0:T(8,128)S(1)} %get-tuple-element.55), channel_id=1, source_target_pairs={{8,0},{16,8},{24,16},{32,24},{40,32},{48,40},{56,48},{64,56},{72,6... | collective-permute-start | bytes 9224 | tf_op jit(solution)/shard_map/ppermute | solution.py:25
  1078.7 11.2 collective-permute-start.132
  1082.4 11.6 %collective-permute-start.133 = (f32[3,1,256]{1,2,0:T(8,128)S(1)}, f32[3,1,256]{1,2,0:T(8,128)S(1)}, u32[]{:S(2)}, u32[]{:S(2)}) collective-permute-start(f32[3,1,256]{1,2,0:T(8,128)S(1)} %get-tuple-element.53), channel_id=1, source_target_pairs={{8,0},{16,8},{24,16},{32,24},{40,32},{48,40},{56,48},{64,56},{72,6... | collective-permute-start | bytes 9224 | tf_op jit(solution)/shard_map/ppermute | solution.py:25
  1105.1 11.5 %collective-permute-start.136 = (f32[3,1,256]{1,2,0:T(8,128)S(1)}, f32[3,1,256]{1,2,0:T(8,128)S(1)}, u32[]{:S(2)}, u32[]{:S(2)}) collective-permute-start(f32[3,1,256]{1,2,0:T(8,128)S(1)} %get-tuple-element.50), channel_id=1, source_target_pairs={{0,8},{8,16},{16,24},{24,32},{32,40},{40,48},{48,56},{56,64},{64,7... | collective-permute-start | bytes 9224 | tf_op jit(solution)/shard_map/ppermute | solution.py:24
  1109.1 11.6 %collective-permute-start.137 = (f32[3,1,256]{1,2,0:T(8,128)S(1)}, f32[3,1,256]{1,2,0:T(8,128)S(1)}, u32[]{:S(2)}, u32[]{:S(2)}) collective-permute-start(f32[3,1,256]{1,2,0:T(8,128)S(1)} %get-tuple-element.51), channel_id=1, source_target_pairs={{8,0},{16,8},{24,16},{32,24},{40,32},{48,40},{56,48},{64,56},{72,6... | collective-permute-start | bytes 9224 | tf_op jit(solution)/shard_map/ppermute | solution.py:25
  1121.5 7.9 collective-permute-start.138
  (124 other events, 1078.7 us)
where the time goes:
time: 1150 us; the launch traced here: 1140 us
  starting transfers between devices  377 us (33%)
  waiting for transfers between devices  362 us (31%)
  local copies, waits for them, and re-layouts  188 us (16%)
  other arithmetic  126 us (11%)
  blocking collectives  63.8 us (6%)
  matrix products  19 us (2%)
    ppermute x70, starting transfers between devices, padded_2(): before = lax.ppermute(last, axis, up)  258 us
    ppermute x70, waiting for transfers between devices, padded_2(): after = lax.ppermute(first, axis, down)  244 us
    ppermute x70, starting transfers between devices, padded_2(): after = lax.ppermute(first, axis, down)  119 us
    reshape x4, local copies, waits for them, and re-layouts, block_mean(): current.reshape(shape[0], shape[1] // 4, 4, shape[2] // 4, 4)  118 us
    ppermute x70, waiting for transfers between devices, padded_2(): before = lax.ppermute(last, axis, up)  117 us
    all_gather x2, blocking collectives, local(): lax.all_gather(partial_value, 'row', axis=1, tiled=True)  43.4 us
    reduce_sum x4, other arithmetic, block_mean(): current.reshape(shape[0], shape[1] // 4, 4, shape[2] // 4, 4)  41.2 us
    add x15, other arithmetic, fine_smooth(): current = current + omega * (sources - fine_apply(current)) / fine_diag  39.6 us
  transfers between devices with their start and end apart: 140, of which 99 were waited for; matrix products, arithmetic and copies ran while one was open for 2% of the time, Pallas kernels for 0%

commit v1 on v0

v1 whole, which is shorter than its diff:
```python
import functools
import math

import jax
import jax.numpy as jnp
import numpy as np
from jax import lax
from jax.experimental import pallas as pl
from jax.experimental.pallas import tpu as pltpu
from jax.sharding import PartitionSpec as P

SWEEPS = 4
SCREEN = 2e-05
SEAM = 0.2
COARSE_SCALE = 0.0625
F32 = jnp.float32
MESH = pl.DeviceIdType.MESH
HIGHEST = lax.Precision.HIGHEST

ROWS, COLS = 512, 256
PAD = 48
HALO = 32
K = (ROWS + 2 * PAD) // 8
NAT = 8 + ROWS + 2 * PAD + 8
LROWS, LCOLS = 128, 64
LPAD = PAD // 4
LHALO = 16
KL = (LROWS + 2 * LPAD) // 8
LNAT = LROWS + 2 * LHALO
CROWS, CCOLS = 32, 16
BROWS = CROWS + 16
VMEM_LIMIT = 62 * 1024 * 1024


def chebyshev_weight(sweep_index):
    return 1.0 / (1.25 + 0.75 * math.cos(math.pi * (2 * sweep_index + 1) / (2 * SWEEPS)))


def lane_iota():
    return lax.broadcasted_iota(jnp.int32, (8, 128), 1)


def sub_iota():
    return lax.broadcasted_iota(jnp.int32, (8, 128), 0)


def lroll(x, shift):
    shift = shift % 128
    return x if shift == 0 else pltpu.roll(x, shift, 1)


def rows8(k):
    return pl.ds(pl.multiple_of(k * 8, 8), 8)


def lanes_take(x, idx):
    return jnp.take_along_axis(x, idx, axis=1)


def left_of(tiles, lane):
    rolled = [lroll(x, 1) for x in tiles]
    return [jnp.where(lane == 0, rolled[(t + 2) % 3], rolled[t]) for t in range(3)]


def right_of(tiles, lane):
    rolled = [lroll(x, 127) for x in tiles]
    return [jnp.where(lane == 127, rolled[(t + 1) % 3], rolled[t]) for t in range(3)]


def set_pads(ref, lead, count):
    last = ref[lead + (rows8(count), slice(None))]
    first = ref[lead + (rows8(1), slice(None))]
    ref[lead + (rows8(0), slice(None))] = pltpu.roll(last, 1, 0)
    ref[lead + (rows8(count + 1), slice(None))] = pltpu.roll(first, 7, 0)


def pack_fine(tile_of, n_arrays, right, left, lane, rows):
    def body(i, carry):
        r = rows8(i)
        for first in range(0, n_arrays, 4):
            out_r = out_l = jnp.zeros((8, 128), F32)
            for a in range(first, min(first + 4, n_arrays)):
                g = a - first
                here = (lane >= 32 * g) & (lane < 32 * g + 32)
                out_r = jnp.where(here, lroll(tile_of(a, 1, r), 32 * g - 96), out_r)
                out_l = jnp.where(here, lroll(tile_of(a, 0, r), 32 * g), out_l)
            right[first // 4, r, :] = out_r
            left[first // 4, r, :] = out_l
        return carry

    lax.fori_loop(0, rows // 8, body, 0)


def unpack_fine(nat, n_arrays, at, count, from_left, from_right, lane):
    def body(i, carry):
        src = rows8(i)
        dst = pl.ds(pl.multiple_of(at + i * 8, 8), 8)
        for a in range(n_arrays):
            g = a % 4
            l = lroll(from_left[a // 4, src, :], 96 - 32 * g)
            r = lroll(from_right[a // 4, src, :], -32 * g)
            nat[a, 2, dst, :] = jnp.where(lane < 32, r, jnp.where(lane >= 96, l, 0.0))
        return carry

    lax.fori_loop(0, count, body, 0)


def zero_ends(nat, n_arrays):
    zero = jnp.zeros((8, 128), F32)
    for a in range(n_arrays):
        for t in range(3):
            for r in (0, 8, 16, NAT - 24, NAT - 16, NAT - 8):
                nat[a, t, r : r + 8, :] = zero


def unpack_columns(nat, n_arrays, cols, corners, lane):
    unpack_fine(nat, n_arrays, 8 + PAD, ROWS // 8, cols.at[0], cols.at[1], lane)
    unpack_fine(nat, n_arrays, 8 + PAD - HALO, HALO // 8, corners.at[0], corners.at[1], lane)
    unpack_fine(nat, n_arrays, 8 + PAD + ROWS, HALO // 8, corners.at[2], corners.at[3], lane)


def fine_inside(k, t, lane, sub, row0, col0, n_rows, n_cols):
    row = row0 - PAD + sub * K + k
    if t < 2:
        col = lane + (col0 + 128 * t)
    else:
        col = jnp.where(lane < 64, lane + (col0 + 256), lane + (col0 - 128))
    return (row >= 0) & (row < n_rows) & (col >= 0) & (col < n_cols), row, col


def level_inside(k, lane, sub, row0, col0, n_rows, n_cols):
    row = row0 - LPAD + sub * KL + k
    col = jnp.where(lane < 96, lane, lane - 128) + col0
    return (row >= 0) & (row < n_rows) & (col >= 0) & (col < n_cols)


def fine_neighbours(v, w, k, lane, ch):
    here = [v[ch, t, rows8(k + 1), :] for t in range(3)]
    left, right = left_of(here, lane), right_of(here, lane)
    total = []
    for t in range(3):
        up, down = v[ch, t, rows8(k), :], v[ch, t, rows8(k + 2), :]
        total.append(w[0][t] * left[t] + w[1][t] * right[t] + w[2][t] * up + w[3][t] * down)
    return here, total


def fine_weights_at(wt, k):
    return [[wt[n, t, rows8(k), :] for t in range(3)] for n in range(4)]


def fine_pads(v):
    for ch in range(3):
        for t in range(3):
            set_pads(v, (ch, t), K)


def fine_sweep(vin, vout, sp, wt, omega):
    lane = lane_iota()

    def body(k, carry):
        w = fine_weights_at(wt, k)
        for ch in range(3):
            here, total = fine_neighbours(vin, w, k, lane, ch)
            for t in range(3):
                new = sp[ch, t, rows8(k), :] + total[t]
                vout[ch, t, rows8(k + 1), :] = (1.0 - omega) * here[t] + omega * new
        return carry

    lax.fori_loop(0, K, body, 0, unroll=2)
    fine_pads(vout)


def fine_first(vout, sp):
    omega = chebyshev_weight(0)

    def body(k, carry):
        for ch in range(3):
            for t in range(3):
                vout[ch, t, rows8(k + 1), :] = omega * sp[ch, t, rows8(k), :]
        return carry

    lax.fori_loop(0, K, body, 0)
    fine_pads(vout)


def fine_smooth(va, vb, sp, wt, from_zero):
    bufs = [va, vb]
    at = 0
    for i in range(SWEEPS):
        if i == 0 and from_zero:
            fine_first(va, sp)
            continue
        fine_sweep(bufs[at], bufs[1 - at], sp, wt, chebyshev_weight(i))
        at = 1 - at
    return bufs[at], bufs[1 - at]


def to_level(x, lane, idx):
    got = []
    for y in x:
        y = y + lroll(y, 127)
        y = y + lroll(y, 126)
        got.append(lanes_take(y, idx))
    return jnp.where(lane < 32, got[0], jnp.where(lane < 64, got[1], got[2]))


def fine_residual_to_level(v, sp, wt, dg, lsrc):
    lane = lane_iota()
    idx = (4 * lane) % 128

    def body(kl, carry):
        acc = [[None] * 3 for _ in range(3)]
        for q in range(4):
            k = kl * 4 + q
            w = fine_weights_at(wt, k)
            for ch in range(3):
                here, total = fine_neighbours(v, w, k, lane, ch)
                for t in range(3):
                    res = dg[t, rows8(k), :] * (sp[ch, t, rows8(k), :] - here[t] + total[t])
                    acc[ch][t] = res if q == 0 else acc[ch][t] + res
        for ch in range(3):
            lsrc[ch, rows8(kl), :] = to_level(acc[ch], lane, idx) * 0.0625
        return carry

    lax.fori_loop(0, KL, body, 0)


def level_weights(fx, fy, lw, ld, li, where):
    lane, sub = lane_iota(), sub_iota()
    fy[rows8(KL), :] = pltpu.roll(fy[rows8(0), :], 7, 0)

    def body(k, carry):
        left, up, down = fx[rows8(k), :], fy[rows8(k), :], fy[rows8(k + 1), :]
        right = lroll(left, 127)
        diag = SCREEN + left + right + up + down
        inv = jnp.where(level_inside(k, lane, sub, *where), 1.0 / diag, 0.0)
        ld[rows8(k), :] = diag
        li[rows8(k), :] = inv
        for n, face in enumerate((left, right, up, down)):
            lw[n, rows8(k), :] = face * inv
        return carry

    lax.fori_loop(0, KL, body, 0)


def level_neighbours(f, lw, k, ch):
    here = f[ch, rows8(k + 1), :]
    total = lw[0, rows8(k), :] * lroll(here, 1) + lw[1, rows8(k), :] * lroll(here, 127)
    return here, total + lw[2, rows8(k), :] * f[ch, rows8(k), :] + lw[3, rows8(k), :] * f[ch, rows8(k + 2), :]


def level_pads(f):
    for ch in range(3):
        set_pads(f, (ch,), KL)


def level_smooth(fa, fb, lsp, lw, from_zero):
    bufs = [fa, fb]
    at = 0
    for i in range(SWEEPS):
        omega = chebyshev_weight(i)
        src, dst = bufs[at], bufs[1 - at]
        if i == 0 and from_zero:

            def first(k, carry):
                for ch in range(3):
                    src[ch, rows8(k + 1), :] = omega * lsp[ch, rows8(k), :]
                return carry

            lax.fori_loop(0, KL, first, 0)
            level_pads(src)
            continue

        def body(k, carry):
            for ch in range(3):
                here, total = level_neighbours(src, lw, k, ch)
                dst[ch, rows8(k + 1), :] = (1.0 - omega) * here + omega * (lsp[ch, rows8(k), :] + total)
            return carry

        lax.fori_loop(0, KL, body, 0)
        level_pads(dst)
        at = 1 - at
    return bufs[at]


def level_down(lsrc, li, ld, lw, lsp, fa, fb, lnat, lev, lpr, lpl, g):
    lane = lane_iota()

    def scale(k, carry):
        for ch in range(3):
            lsp[ch, rows8(k), :] = lsrc[ch, rows8(k), :] * li[rows8(k), :]
        return carry

    lax.fori_loop(0, KL, scale, 0)
    f = level_smooth(fa, fb, lsp, lw, True)

    def out(k, carry):
        at = pl.ds(LHALO - LPAD + k, 8, stride=KL)
        for ch in range(3):
            here, total = level_neighbours(f, lw, k, ch)
            lnat[8 + ch, at, :] = ld[rows8(k), :] * (lsp[ch, rows8(k), :] - here + total)
            lnat[ch, at, :] = here
            lnat[3 + ch, at, :] = lsrc[ch, rows8(k), :]
        return carry

    lax.fori_loop(0, KL, out, 0)

    def copy(i, carry):
        src = pl.ds(pl.multiple_of(LHALO + i * 8, 8), 8)
        right = left = jnp.zeros((8, 128), F32)
        for a in range(8):
            x = lnat[a, src, :]
            lev[a, rows8(i), :] = x
            here = (lane >= 16 * a) & (lane < 16 * a + 16)
            right = jnp.where(here, lroll(x, 16 * a - 48), right)
            left = jnp.where(here, lroll(x, 16 * a), left)
        lpr[rows8(i), :] = right
        lpl[rows8(i), :] = left
        return carry

    lax.fori_loop(0, LROWS // 8, copy, 0)
    idx = (4 * lane) % 128
    for i in range(CROWS // 8):
        total = jnp.zeros((8, 128), F32)
        for ch in range(3):
            x = sum(lnat[8 + ch, pl.ds(LHALO + 32 * i + q, 8, stride=4), :] for q in range(4))
            x = x + lroll(x, 127)
            x = x + lroll(x, 126)
            x = jnp.where(lane < CCOLS, lanes_take(x, idx), 0.0) * 0.0625
            total = total + lroll(x, CCOLS * ch)
        g[i * 8 : i * 8 + 8, :] = total


def level_up(lev, lrows, lcols, lcorn, corr, lnat, lnc, fx, fy, lw, ld, li, lsp, fa, fb, where):
    lane, sub = lane_iota(), sub_iota()

    def place(dst_row, count, own, left, right):
        def body(i, carry):
            dst = pl.ds(pl.multiple_of(dst_row + i * 8, 8), 8)
            l, r = left(rows8(i)), right(rows8(i))
            for a in range(8):
                x = jnp.where(lane < 64, own(a, rows8(i)), 0.0)
                x = jnp.where((lane >= 64) & (lane < 80), lroll(r, 64 - 16 * a), x)
                lnat[a, dst, :] = jnp.where(lane >= 112, lroll(l, 112 - 16 * a), x)
            return carry

        lax.fori_loop(0, count, body, 0)

    place(0, LHALO // 8, lambda a, r: lrows[0, a, r, :], lambda r: lcorn[0, r, :], lambda r: lcorn[1, r, :])
    place(LHALO, LROWS // 8, lambda a, r: lev[a, r, :], lambda r: lcols[0, r, :], lambda r: lcols[1, r, :])
    place(LHALO + LROWS, LHALO // 8, lambda a, r: lrows[1, a, r, :], lambda r: lcorn[2, r, :], lambda r: lcorn[3, r, :])
    for ch in range(3):
        for h in range(LNAT // 32):
            x = corr[ch, 4 + 8 * h : 12 + 8 * h, :]
            for q in range(4):
                lnc[ch, pl.ds(32 * h + q, 8, stride=4), :] = x

    def faces(k, carry):
        at = pl.ds(LHALO - LPAD + k, 8, stride=KL)
        fx[rows8(k), :] = lnat[6, at, :]
        fy[rows8(k), :] = lnat[7, at, :]
        return carry

    lax.fori_loop(0, KL, faces, 0)
    level_weights(fx, fy, lw, ld, li, where)

    def fields(k, carry):
        at = pl.ds(LHALO - LPAD + k, 8, stride=KL)
        inside = level_inside(k, lane, sub, *where)
        inv = li[rows8(k), :]
        for ch in range(3):
            fa[ch, rows8(k + 1), :] = jnp.where(inside, lnat[ch, at, :] + lnc[ch, at, :], 0.0)
            lsp[ch, rows8(k), :] = lnat[3 + ch, at, :] * inv
        return carry

    lax.fori_loop(0, KL, fields, 0)
    level_pads(fa)
    return level_smooth(fa, fb, lsp, lw, False)


def fine_up(v, vrows, vcols, vcorn, field, nat, va, where):
    lane, sub = lane_iota(), sub_iota()
    zero_ends(nat, 3)
    for ch in range(3):
        for t in range(2):
            nat[ch, t, 8 + PAD : 8 + PAD + ROWS, :] = v[ch, t]
            nat[ch, t, 8 + PAD - HALO : 8 + PAD, :] = vrows[0, ch, t]
            nat[ch, t, 8 + PAD + ROWS : 8 + PAD + ROWS + HALO, :] = vrows[1, ch, t]
    unpack_columns(nat, 3, vcols, vcorn, lane)
    quarter = lane // 4
    idx = [quarter, 32 + quarter, jnp.where(lane < 64, 64 + quarter, 96 + quarter)]

    def body(kl, carry):
        for ch in range(3):
            level = field[ch, rows8(kl + 1), :]
            for t in range(3):
                add = lanes_take(level, idx[t])
                for q in range(4):
                    k = kl * 4 + q
                    inside = fine_inside(k, t, lane, sub, *where)[0]
                    x = nat[ch, t, pl.ds(8 + k, 8, stride=K), :] + add
                    va[ch, t, rows8(k + 1), :] = jnp.where(inside, x, 0.0)
        return carry

    lax.fori_loop(0, KL, body, 0)
    fine_pads(va)


def field_out(field, nat, v, vpr, vpl):
    lane = lane_iota()

    def body(k, carry):
        for ch in range(3):
            for t in range(2):
                nat[ch, t, pl.ds(8 + k, 8, stride=K), :] = field[ch, t, rows8(k + 1), :]
        return carry

    lax.fori_loop(0, K, body, 0)
    for ch in range(3):
        for t in range(2):
            v[ch, t] = nat[ch, t, 8 + PAD : 8 + PAD + ROWS, :]
    pack_fine(lambda a, t, r: v[a, t, r, :], 3, vpr, vpl, lane, ROWS)


def positions(n_row, n_col):
    i, j = lax.axis_index("row"), lax.axis_index("col")
    fine = (i * ROWS, j * COLS, n_row * ROWS, n_col * COLS)
    level = (i * LROWS, j * LCOLS, n_row * LROWS, n_col * LCOLS)
    return fine, level


def start_kernel(
    n_row, n_col,
    src, codes, labels, srows, crows, lrows, cols, corners,
    sp, wt, dg, v, vpr, vpl, lev, lpr, lpl, g,
    nat, fxp, fyp, va, vb, lsrc, lfx, lfy, lw, ld, li, lsp, fa, fb, lnat,
):
    where, lwhere = positions(n_row, n_col)
    lane, sub = lane_iota(), sub_iota()
    zero_ends(nat, 6)
    mid, top, low = (
        pl.ds(8 + PAD, ROWS),
        pl.ds(8 + PAD - HALO, HALO),
        pl.ds(8 + PAD + ROWS, HALO),
    )
    for t in range(2):
        c = slice(128 * t, 128 * t + 128)
        for a in range(3):
            nat[a, t, mid, :] = src[a, :, c]
            nat[a, t, top, :] = srows[0, a, :, c]
            nat[a, t, low, :] = srows[1, a, :, c]
        for a in range(2):
            nat[3 + a, t, mid, :] = codes[a, :, c].astype(F32)
            nat[3 + a, t, top, :] = crows[0, a, :, c].astype(F32)
            nat[3 + a, t, low, :] = crows[1, a, :, c].astype(F32)
        nat[5, t, mid, :] = labels[:, c].astype(F32)
        nat[5, t, top, :] = lrows[0, :, c].astype(F32)
        nat[5, t, low, :] = lrows[1, :, c].astype(F32)
    unpack_columns(nat, 6, cols, corners, lane)

    def edge(code, a, b):
        return jnp.exp2(code * 0.25 - 2.0) * jnp.where(a != b, SEAM, 1.0)

    def faces(k, carry):
        at, above = pl.ds(8 + k, 8, stride=K), pl.ds(7 + k, 8, stride=K)
        code = left_of([nat[3, t, at, :] for t in range(3)], lane)
        label = [nat[5, t, at, :] for t in range(3)]
        beside = left_of(label, lane)
        for t in range(3):
            _, row, col = fine_inside(k, t, lane, sub, *where)
            inner = edge(code[t], beside[t], label[t])
            fxp[t, rows8(k), :] = jnp.where((col >= 1) & (col < where[3]), inner, 1.0)
            inner = edge(nat[4, t, above, :], nat[5, t, above, :], label[t])
            fyp[t, rows8(k), :] = jnp.where((row >= 1) & (row < where[2]), inner, 1.0)
        return carry

    lax.fori_loop(0, K, faces, 0)
    for t in range(3):
        fyp[t, rows8(K), :] = pltpu.roll(fyp[t, rows8(0), :], 7, 0)

    def weights(k, carry):
        left = [fxp[t, rows8(k), :] for t in range(3)]
        right = right_of(left, lane)
        at = pl.ds(8 + k, 8, stride=K)
        for t in range(3):
            up, down = fyp[t, rows8(k), :], fyp[t, rows8(k + 1), :]
            diag = SCREEN + left[t] + right[t] + up + down
            inside = fine_inside(k, t, lane, sub, *where)[0]
            inv = jnp.where(inside, 1.0 / diag, 0.0)
            dg[t, rows8(k), :] = diag
            for n, face in enumerate((left[t], right[t], up, down)):
                wt[n, t, rows8(k), :] = face * inv
            for ch in range(3):
                sp[ch, t, rows8(k), :] = nat[ch, t, at, :] * inv
        return carry

    lax.fori_loop(0, K, weights, 0)
    idx = (4 * lane) % 128

    def level_faces(kl, carry):
        got = [
            lanes_take(sum(fxp[t, rows8(kl * 4 + q), :] for q in range(4)), idx) for t in range(3)
        ]
        x = jnp.where(lane < 32, got[0], jnp.where(lane < 64, got[1], got[2])) * 0.0625
        y = to_level([fyp[t, rows8(kl * 4), :] for t in range(3)], lane, idx) * 0.0625
        at = pl.ds(LHALO - LPAD + kl, 8, stride=KL)
        lfx[rows8(kl), :] = x
        lfy[rows8(kl), :] = y
        lnat[6, at, :] = x
        lnat[7, at, :] = y
        return carry

    lax.fori_loop(0, KL, level_faces, 0)
    level_weights(lfx, lfy, lw, ld, li, lwhere)
    field, _ = fine_smooth(va, vb, sp, wt, True)
    fine_residual_to_level(field, sp, wt, dg, lsrc)
    level_down(lsrc, li, ld, lw, lsp, fa, fb, lnat, lev, lpr, lpl, g)
    field_out(field, nat, v, vpr, vpl)


def cycle_kernel(
    n_row, n_col,
    sp, wt, dg, v_in, vrows, vcols, vcorn, lev_in, lrows, lcols, lcorn, corr,
    v, vpr, vpl, lev, lpr, lpl, g,
    nat, va, vb, lsrc, lfx, lfy, lw, ld, li, lsp, fa, fb, lnat, lnc,
):
    where, lwhere = positions(n_row, n_col)
    level = level_up(
        lev_in, lrows, lcols, lcorn, corr, lnat, lnc, lfx, lfy, lw, ld, li, lsp, fa, fb, lwhere
    )
    fine_up(v_in, vrows, vcols, vcorn, level, nat, va, where)
    field, other = fine_smooth(va, vb, sp, wt, False)
    field, other = fine_smooth(field, other, sp, wt, False)
    fine_residual_to_level(field, sp, wt, dg, lsrc)
    level_down(lsrc, li, ld, lw, lsp, fa, fb, lnat, lev, lpr, lpl, g)
    field_out(field, nat, v, vpr, vpl)


def end_kernel(
    n_row, n_col,
    sp, wt, dg, v_in, vrows, vcols, vcorn, lev_in, lrows, lcols, lcorn, corr,
    solution_out, residual_out,
    nat, va, vb, lfx, lfy, lw, ld, li, lsp, fa, fb, lnat, lnc,
):
    where, lwhere = positions(n_row, n_col)
    lane = lane_iota()
    level = level_up(
        lev_in, lrows, lcols, lcorn, corr, lnat, lnc, lfx, lfy, lw, ld, li, lsp, fa, fb, lwhere
    )
    fine_up(v_in, vrows, vcols, vcorn, level, nat, va, where)
    field, _ = fine_smooth(va, vb, sp, wt, False)

    def body(k, carry):
        at = pl.ds(8 + k, 8, stride=K)
        w = fine_weights_at(wt, k)
        for ch in range(3):
            here, total = fine_neighbours(field, w, k, lane, ch)
            for t in range(2):
                nat[ch, t, at, :] = here[t]
                res = dg[t, rows8(k), :] * (sp[ch, t, rows8(k), :] - here[t] + total[t])
                nat[3 + ch, t, at, :] = res
        return carry

    lax.fori_loop(0, K, body, 0)
    for ch in range(3):
        for t in range(2):
            c = slice(128 * t, 128 * t + 128)
            solution_out[ch, :, c] = nat[ch, t, 8 + PAD : 8 + PAD + ROWS, :]
            residual_out[ch, :, c] = nat[3 + ch, t, 8 + PAD : 8 + PAD + ROWS, :]


def around(n_row, n_col):
    i, j = lax.axis_index("row"), lax.axis_index("col")
    up, down = lax.rem(i + n_row - 1, n_row), lax.rem(i + 1, n_row)
    left, right = lax.rem(j + n_col - 1, n_col), lax.rem(j + 1, n_col)
    return i, j, up, down, left, right


def send(copies, src, dst, sems, device):
    n = len(copies)
    copy = pltpu.make_async_remote_copy(
        src_ref=src, dst_ref=dst, send_sem=sems[0].at[n], recv_sem=sems[1].at[n],
        device_id=device, device_id_type=MESH,
    )
    copy.start()
    copies.append(copy)
    return copy


def exchange_kernel(
    n_row, n_col,
    src, codes, labels, src_v, codes_v, labels_v,
    srows, crows, lrows, cols, corners,
    right_pack, left_pack, send_sems, recv_sems,
):
    i, j, up, down, left, right = around(n_row, n_col)
    barrier = pltpu.get_barrier_semaphore()
    for r in (up, i, down):
        for c in (left, j, right):
            if r is not i or c is not j:
                pl.semaphore_signal(barrier, inc=1, device_id=(r, c), device_id_type=MESH)
    lane = lane_iota()

    def tile_of(a, t, r):
        c = slice(128 * t, 128 * t + 128)
        if a < 3:
            return src_v[a, r, c]
        if a < 5:
            return codes_v[a - 3, r, c].astype(F32)
        return labels_v[r, c].astype(F32)

    pack_fine(tile_of, 6, right_pack, left_pack, lane, ROWS)
    pl.semaphore_wait(barrier, 8)
    copies, sems = [], (send_sems, recv_sems)
    top, low = pl.ds(0, HALO), pl.ds(ROWS - HALO, HALO)
    send(copies, right_pack, cols.at[0], sems, (i, right))
    send(copies, left_pack, cols.at[1], sems, (i, left))
    for slot, rows, device in ((1, top, up), (0, low, down)):
        send(copies, src.at[:, rows, :], srows.at[slot], sems, (device, j))
        send(copies, codes.at[:, rows, :], crows.at[slot], sems, (device, j))
        send(copies, labels.at[rows, :], lrows.at[slot], sems, (device, j))
    send(copies, right_pack.at[:, low, :], corners.at[0], sems, (down, right))
    send(copies, left_pack.at[:, low, :], corners.at[1], sems, (down, left))
    send(copies, right_pack.at[:, top, :], corners.at[2], sems, (up, right))
    send(copies, left_pack.at[:, top, :], corners.at[3], sems, (up, left))
    for copy in copies:
        copy.wait()


def coarse_kernel(
    n_row, n_col,
    g, s_cols, s_rows, t_back, row_eig, col_eig, s_ext, v, vpr, vpl, lev, lpr, lpl,
    vrows, vcols, vcorn, lrows, lcols, lcorn, corr,
    one, two, three, mine, spec, back, send_sems, recv_sems,
):
    i, j, up, down, left, right = around(n_row, n_col)
    n_modes = n_row * CROWS
    barrier = pltpu.get_barrier_semaphore()
    for d in range(1, n_col):
        pl.semaphore_signal(barrier, inc=1, device_id=(i, lax.rem(j + d, n_col)), device_id_type=MESH)
    for d in range(1, n_row):
        pl.semaphore_signal(barrier, inc=1, device_id=(lax.rem(i + d, n_row), j), device_id_type=MESH)
    for r in (up, down):
        for c in (left, right):
            pl.semaphore_signal(barrier, inc=1, device_id=(r, c), device_id_type=MESH)
    pl.semaphore_wait(barrier, n_col + n_row + 2)
    copies, sems = [], (send_sems, recv_sems)
    lane = lane_iota()

    first = [
        send(copies, g, one.at[j], sems, (i, lax.rem(j + d, n_col))) for d in range(1, n_col)
    ]
    one[j] = g[...]
    halos = []
    top, low = pl.ds(0, HALO), pl.ds(ROWS - HALO, HALO)
    ltop, llow = pl.ds(0, LHALO), pl.ds(LROWS - LHALO, LHALO)

    def halo(*args):
        halos.append(send(copies, *args[:2], sems, args[2]))

    halo(lpr, lcols.at[0], (i, right))
    halo(lpl, lcols.at[1], (i, left))
    halo(lev.at[:, ltop, :], lrows.at[1], (up, j))
    halo(lev.at[:, llow, :], lrows.at[0], (down, j))
    halo(lpr.at[llow, :], lcorn.at[0], (down, right))
    halo(lpl.at[llow, :], lcorn.at[1], (down, left))
    halo(lpr.at[ltop, :], lcorn.at[2], (up, right))
    halo(lpl.at[ltop, :], lcorn.at[3], (up, left))
    for copy in first:
        copy.wait()

    def placed(ref, n_rows):
        out = []
        for ch in range(3):
            parts = []
            for r in range(n_rows // 8):
                x = jnp.zeros((8, 128), F32)
                for p in range(n_col):
                    here = (lane >= CCOLS * p) & (lane < CCOLS * p + CCOLS)
                    y = lroll(ref[p, r * 8 : r * 8 + 8, :], CCOLS * (p - ch))
                    x = jnp.where(here, y, x)
                parts.append(x)
            out.append(jnp.concatenate(parts, axis=0))
        return out

    x = jnp.concatenate(placed(one, CROWS), axis=0)
    x = jnp.dot(x, s_cols[j], precision=HIGHEST, preferred_element_type=F32)
    total = lax.slice_in_dim(x, 0, CROWS)
    for ch in (1, 2):
        total = total + pltpu.roll(lax.slice_in_dim(x, CROWS * ch, CROWS * ch + CROWS), CCOLS * ch, 1)
    mine[...] = total
    own = pl.ds(pl.multiple_of(i * CROWS, CROWS), CROWS)
    second = [
        send(copies, mine, two.at[own, :], sems, (lax.rem(i + d, n_row), j)) for d in range(1, n_row)
    ]
    two[own, :] = total
    halo(vpr, vcols.at[0], (i, right))
    halo(vpl, vcols.at[1], (i, left))
    halo(vpr.at[:, low, :], vcorn.at[0], (down, right))
    halo(vpl.at[:, low, :], vcorn.at[1], (down, left))
    halo(vpr.at[:, top, :], vcorn.at[2], (up, right))
    halo(vpl.at[:, top, :], vcorn.at[3], (up, left))
    for copy in second:
        copy.wait()
    halo(v.at[:, :, top, :], vrows.at[1], (up, j))
    halo(v.at[:, :, low, :], vrows.at[0], (down, j))
    y = jnp.dot(s_rows[...], two[...], precision=HIGHEST, preferred_element_type=F32)
    eig = SCREEN + COARSE_SCALE * (row_eig[...] + col_eig[pl.ds(j, 1), :])
    spec[...] = y / eig
    rows = s_ext[pl.ds(pl.multiple_of(i * CROWS, CROWS), BROWS), :]
    z = jnp.dot(rows, spec[...], precision=HIGHEST, preferred_element_type=F32)
    back[...] = z
    third = [
        send(copies, back, three.at[j], sems, (i, lax.rem(j + d, n_col))) for d in range(1, n_col)
    ]
    three[j] = z
    for copy in third:
        copy.wait()
    z = jnp.concatenate(placed(three, BROWS), axis=0)
    z = jnp.dot(z, t_back[j], precision=HIGHEST, preferred_element_type=F32)
    for ch in range(3):
        corr[ch] = lax.slice_in_dim(z, BROWS * ch, BROWS * ch + BROWS)
    for copy in halos:
        copy.wait()


@functools.lru_cache(maxsize=None)
def tables(n_row, n_col):
    def sines(n):
        k = np.arange(1, n + 1)
        return math.sqrt(2.0 / (n + 1)) * np.sin(np.pi * ((k[:, None] * k[None, :]) % (2 * (n + 1))) / (n + 1))

    def eig(n):
        return 2.0 - 2.0 * np.cos(np.pi * np.arange(1, n + 1) / (n + 1))

    nr, nc = n_row * CROWS, n_col * CCOLS
    rows, cols = sines(nr), sines(nc)
    s_cols = np.zeros((n_col, 128, 128))
    t_back = np.zeros((n_col, 128, 128))
    col_eig = np.ones((n_col, 128))
    lane = np.arange(128)
    for j in range(n_col):
        own = slice(CCOLS * j, CCOLS * j + CCOLS)
        s_cols[j, :nc, :CCOLS] = cols[:, own]
        col_eig[j, : 3 * CCOLS] = np.tile(eig(nc)[own], 3)
        c = LCOLS * j + np.where(lane < 96, lane, lane - 128)
        ok = (c >= 0) & (c < n_col * LCOLS) & ((lane < 80) | (lane >= 112))
        t_back[j, :nc, ok] = cols[:, c[ok] // 4].T
    s_ext = np.zeros((nr + 16, nr))
    s_ext[8 : 8 + nr] = rows
    row_eig = np.repeat(eig(nr)[:, None], 128, axis=1)
    return tuple(x.astype(np.float32) for x in (s_cols, rows, t_back, row_eig, col_eig, s_ext))


def shape(*dims, dtype=F32):
    return jax.ShapeDtypeStruct(dims, dtype)


IN_VMEM = pl.BlockSpec(memory_space=pltpu.VMEM)
IN_ANY = pl.BlockSpec(memory_space=pl.ANY)


def solution(mesh):
    n_row, n_col = mesh.shape["row"], mesh.shape["col"]
    fine = functools.partial(pltpu.VMEM, dtype=F32)
    params = pltpu.CompilerParams(vmem_limit_bytes=VMEM_LIMIT)

    def level_scratch():
        flat = pltpu.VMEM((KL * 8, 128), F32)
        padded = pltpu.VMEM((3, (KL + 2) * 8, 128), F32)
        return [
            flat, pltpu.VMEM(((KL + 1) * 8, 128), F32), pltpu.VMEM((4, KL * 8, 128), F32), flat, flat,
            pltpu.VMEM((3, KL * 8, 128), F32), padded, padded, pltpu.VMEM((11, LNAT, 128), F32),
        ]

    padded = pltpu.VMEM((3, 3, (K + 2) * 8, 128), F32)
    lsrc = pltpu.VMEM((3, KL * 8, 128), F32)
    lnc = pltpu.VMEM((3, LNAT, 128), F32)
    nat = lambda n: pltpu.VMEM((n, 3, NAT, 128), F32)
    down_shapes = [
        shape(3, 2, ROWS, 128), shape(1, ROWS, 128), shape(1, ROWS, 128), shape(8, LROWS, 128),
        shape(LROWS, 128), shape(LROWS, 128), shape(CROWS, 128),
    ]
    n_coarse = 2 * (n_col - 1) + (n_row - 1) + 16

    def call(kernel, n_in, outs, scratch):
        return pl.pallas_call(
            functools.partial(kernel, n_row, n_col), out_shape=outs, in_specs=[IN_VMEM] * n_in,
            out_specs=[IN_VMEM] * len(outs), scratch_shapes=scratch, compiler_params=params,
        )

    exchange = pl.pallas_call(
        functools.partial(exchange_kernel, n_row, n_col),
        out_shape=[
            shape(2, 3, HALO, COLS), shape(2, 2, HALO, COLS, dtype=jnp.int32), shape(2, HALO, COLS, dtype=jnp.int32),
            shape(2, 2, ROWS, 128), shape(4, 2, HALO, 128),
        ],
        in_specs=[IN_ANY] * 3 + [IN_VMEM] * 3,
        out_specs=[IN_VMEM] * 5,
        scratch_shapes=[pltpu.VMEM((2, ROWS, 128), F32)] * 2 + [pltpu.SemaphoreType.DMA((12,))] * 2,
        compiler_params=pltpu.CompilerParams(collective_id=0, has_side_effects=True, vmem_limit_bytes=VMEM_LIMIT),
    )
    start = call(
        start_kernel, 8,
        [shape(3, 3, K * 8, 128), shape(4, 3, K * 8, 128), shape(3, K * 8, 128)] + down_shapes,
        [nat(6), pltpu.VMEM((3, K * 8, 128), F32), pltpu.VMEM((3, (K + 1) * 8, 128), F32), padded, padded, lsrc]
        + level_scratch(),
    )
    coarse = pl.pallas_call(
        functools.partial(coarse_kernel, n_row, n_col),
        out_shape=[
            shape(2, 3, 2, HALO, 128), shape(2, 1, ROWS, 128), shape(4, 1, HALO, 128),
            shape(2, 8, LHALO, 128), shape(2, LROWS, 128), shape(4, LHALO, 128), shape(3, BROWS, 128),
        ],
        in_specs=[IN_VMEM] * 7 + [IN_ANY] * 6,
        out_specs=[IN_VMEM] * 7,
        scratch_shapes=[
            pltpu.VMEM((n_col, CROWS, 128), F32), pltpu.VMEM((n_row * CROWS, 128), F32),
            pltpu.VMEM((n_col, BROWS, 128), F32), pltpu.VMEM((CROWS, 128), F32),
            pltpu.VMEM((n_row * CROWS, 128), F32), pltpu.VMEM((BROWS, 128), F32),
            pltpu.SemaphoreType.DMA((n_coarse,)), pltpu.SemaphoreType.DMA((n_coarse,)),
        ],
        compiler_params=pltpu.CompilerParams(collective_id=1, has_side_effects=True, vmem_limit_bytes=VMEM_LIMIT),
    )
    cycle = call(cycle_kernel, 12, down_shapes, [nat(3), padded, padded, lsrc] + level_scratch() + [lnc])
    end = call(
        end_kernel, 12, [shape(3, ROWS, COLS)] * 2, [nat(6), padded, padded] + level_scratch() + [lnc]
    )
    consts = tables(n_row, n_col)

    def local(sources, edge_codes, seam_labels):
        halos = exchange(sources, edge_codes, seam_labels, sources, edge_codes, seam_labels)
        sp, wt, dg, *down = start(sources, edge_codes, seam_labels, *halos)
        for step in (cycle, end):
            v, vpr, vpl, lev, lpr, lpl, g = down
            vrows, vcols, vcorn, lrows, lcols, lcorn, corr = coarse(g, *consts, v, vpr, vpl, lev, lpr, lpl)
            down = step(sp, wt, dg, v, vrows, vcols, vcorn, lev, lrows, lcols, lcorn, corr)
        return tuple(down)

    spec = P(None, "row", "col")
    return jax.shard_map(
        local, mesh=mesh, in_specs=(spec, spec, P("row", "col")), out_specs=(spec, spec), check_vma=False
    )
```

time: 1150 us -> 263 us (0.23)
  starting transfers between devices: 377 us -> 0 us
  waiting for transfers between devices: 362 us -> 0 us
  Pallas kernels: 0 us -> 263 us
  local copies, waits for them, and re-layouts: 188 us -> 0 us
  other arithmetic: 126 us -> 0 us
  blocking collectives: 63.8 us -> 0 us
  matrix products: 19 us -> 0 us
    ppermute x140 -> x0, starting transfers between devices: 377 us -> none  [the longest x70 258 us: padded_2(): before = lax.ppermute(last, axis, up)]
    ppermute x140 -> x0, waiting for transfers between devices: 362 us -> none  [the longest x70 244 us: padded_2(): after = lax.ppermute(first, axis, down)]
    pallas_call x0 -> x6, Pallas kernels: none -> 263 us  [the longest x2 125 us: local(): step(sp, wt, dg, v, vrows, vcols, vcorn, lev, lrows, lcols, lcorn, corr)]
    reshape x13 -> x0, local copies, waits for them, and re-layouts: 136 us -> none  [the longest x4 118 us: block_mean(): current.reshape(shape[0], shape[1] // 4, 4, shape[2] // 4, 4)]
    all_gather x4 -> x0, blocking collectives: 63.8 us -> none  [the longest x2 43.4 us: local(): lax.all_gather(partial_value, 'row', axis=1, tiled=True)]
    add x38 -> x0, other arithmetic: 53.4 us -> none  [the longest x15 39.6 us: fine_smooth(): current = current + omega * (sources - fine_apply(current)) / fine_diag]
    reduce_sum x6 -> x0, other arithmetic: 44.6 us -> none  [the longest x4 41.2 us: block_mean(): current.reshape(shape[0], shape[1] // 4, 4, shape[2] // 4, 4)]
    dot_general x8 -> x0, matrix products: 19 us -> none  [the longest x2 15 us: local(): jnp.einsum('ki,cij->ckj', table_rows, lax.all_gather(partial_value, 'row'...]
  transfers between devices with their start and end apart: 140 -> 0, of which waited for: 99 -> 0; matrix products, arithmetic and copies ran while one was open for 2% -> 0% of each run, Pallas kernels for 0% -> 0%
where the time goes in v1:
time: 263 us
  Pallas kernels  263 us (100%)
    pallas_call x2, Pallas kernels, local(): step(sp, wt, dg, v, vrows, vcols, vcorn, lev, lrows, lcols, lcorn, corr)  125 us
    pallas_call x1, Pallas kernels, local(): sp, wt, dg, *down = start(sources, edge_codes, seam_labels, *halos)  65.4 us
    pallas_call x2, Pallas kernels, local(): coarse(g, *consts, v, vpr, vpl, lev, lpr, lpl)  48.8 us
    pallas_call x1, Pallas kernels, local(): exchange(sources, edge_codes, seam_labels, sources, edge_codes, seam_labels)  23.1 us

profile of v1, /device:TPU:1, one launch (start us, length us, event | category | flops | bytes accessed | tf_op | source)
XLA Modules:
  0.0 263.3 jit_solution(14160764745070546347)
XLA Ops:
  0.6 23.1 %shard_map.104 = (f32[2,3,32,256]{3,2,1,0:T(8,128)}, s32[2,2,32,256]{3,2,1,0:T(8,128)}, s32[2,32,256]{2,1,0:T(8,128)}, f32[2,2,512,128]{3,2,1,0:T(8,128)}, f32[4,2,32,128]{3,2,1,0:T(8,128)}) custom-call(f32[3,512,256]{2,1,0:T(8,128)} %src.3, s32[2,512,256]{2,1,0:T(8,128)} %codes.3, s32[512,256]{1,0:T(8,128)} %labels.3, f32[3,512,256]{2,1,0:T(8,128)} %src.3, ...), custom_call_target="tpu_custom_call" | custom-call | tf_op jit(solution)/shard_map/pallas_call | solution.py:832
  23.7 65.4 %shard_map.105 = (f32[3,3,608,128]{3,2,1,0:T(8,128)}, f32[4,3,608,128]{3,2,1,0:T(8,128)}, f32[3,608,128]{2,1,0:T(8,128)}, f32[3,2,512,128]{3,2,1,0:T(8,128)}, f3...) custom-call(f32[3,512,256]{2,1,0:T(8,128)} %src.3, ...), custom_call_target="tpu_custom_call" | custom-call | tf_op jit(solution)/shard_map/pallas_call | solution.py:833
  89.1 24.3 %shard_map.106 = (f32[2,3,2,32,128]{4,3,2,1,0:T(8,128)}, f32[2,1,512,128]{3,2,1,0:T(8,128)}, f32[4,1,32,128]{3,2,1,0:T(8,128)}, f32[2,8,16,128]{3,2,1,0:T(8,128)...) custom-call(f32[32,128]{1,0:T(8,128)} %get-tuple-element.47.g, ...), custom_call_target="tpu_custom_call" | custom-call | tf_op jit(solution)/shard_map/pallas_call | solution.py:836
  113.4 77.8 %shard_map.107 = (f32[3,2,512,128]{3,2,1,0:T(8,128)}, f32[1,512,128]{2,1,0:T(8,128)}, f32[1,512,128]{2,1,0:T(8,128)}, f32[8,128,128]{2,1,0:T(8,128)}, f32[128,12...) custom-call(f32[3,3,608,128]{3,2,1,0:T(8,128)} %get-tuple-element.43.sp, ...), custom_call_target="tpu_custom_call" | custom-call | tf_op jit(solution)/shard_map/pallas_call | solution.py:837
  191.2 24.5 %shard_map.108 = (f32[2,3,2,32,128]{4,3,2,1,0:T(8,128)}, f32[2,1,512,128]{3,2,1,0:T(8,128)}, f32[4,1,32,128]{3,2,1,0:T(8,128)}, f32[2,8,16,128]{3,2,1,0:T(8,128)...) custom-call(f32[32,128]{1,0:T(8,128)} %get-tuple-element.61.g, ...), custom_call_target="tpu_custom_call" | custom-call | tf_op jit(solution)/shard_map/pallas_call | solution.py:836
  215.7 47.6 %shard_map.109 = (f32[3,512,256]{2,1,0:T(8,128)}, f32[3,512,256]{2,1,0:T(8,128)}) custom-call(f32[3,3,608,128]{3,2,1,0:T(8,128)} %get-tuple-element.43.sp, f32[4,3,608,128]{3,2,1,0:T(8,128)} %get-tuple-element.44.wt, f32[3,608,128]{2,1,0:T(8,128)} %get-tuple-element.45.dg, f32[3,2,512,128]{3,2,1,0:T(8,128)} %get-tuple-element.60.v.v_in, ...), custom_call_target="tpu_custom_call" | custom-call | tf_op jit(solution)/shard_map/pallas_call | solution.py:837

commit v2 on v1

--- a/solution.py
+++ b/solution.py
@@ -134,18 +134,44 @@
     return (row >= 0) & (row < n_rows) & (col >= 0) & (col < n_cols)
 
 
-def fine_neighbours(v, w, k, lane, ch):
-    here = [v[ch, t, rows8(k + 1), :] for t in range(3)]
-    left, right = left_of(here, lane), right_of(here, lane)
-    total = []
-    for t in range(3):
-        up, down = v[ch, t, rows8(k), :], v[ch, t, rows8(k + 2), :]
-        total.append(w[0][t] * left[t] + w[1][t] * right[t] + w[2][t] * up + w[3][t] * down)
-    return here, total
-
-
-def fine_weights_at(wt, k):
-    return [[wt[n, t, rows8(k), :] for t in range(3)] for n in range(4)]
+def stencil_pass(v, wt, sl, emit, tiles=3, begin=None, end=None):
+    lane = lane_iota()
+
+    def shift(k, slot):
+        for ch in range(3):
+            here = [v[ch, t, rows8(k + 1), :] for t in range(3)]
+            left, right = left_of(here, lane), right_of(here, lane)
+            for t in range(3):
+                sl[slot, 0, ch, t] = left[t]
+                sl[slot, 1, ch, t] = right[t]
+
+    def compute(k, slot):
+        for t in range(tiles):
+            w = [wt[n, t, rows8(k), :] for n in range(4)]
+            for ch in range(3):
+                total = w[0] * sl[slot, 0, ch, t] + w[1] * sl[slot, 1, ch, t]
+                total = total + w[2] * v[ch, t, rows8(k), :] + w[3] * v[ch, t, rows8(k + 2), :]
+                emit(k, ch, t, v[ch, t, rows8(k + 1), :], total)
+
+    def body(m, carry):
+        k = 4 * m
+        if begin is not None:
+            begin()
+        shift(k + 2, 2)
+        shift(k + 3, 3)
+        compute(k, 0)
+        compute(k + 1, 1)
+        shift(k + 4, 0)
+        shift(k + 5, 1)
+        compute(k + 2, 2)
+        compute(k + 3, 3)
+        if end is not None:
+            end(m)
+        return carry
+
+    shift(0, 0)
+    shift(1, 1)
+    lax.fori_loop(0, K // 4, body, 0)
 
 
 def fine_pads(v):
@@ -154,19 +180,12 @@
             set_pads(v, (ch, t), K)
 
 
-def fine_sweep(vin, vout, sp, wt, omega):
-    lane = lane_iota()
-
-    def body(k, carry):
-        w = fine_weights_at(wt, k)
-        for ch in range(3):
-            here, total = fine_neighbours(vin, w, k, lane, ch)
-            for t in range(3):
-                new = sp[ch, t, rows8(k), :] + total[t]
-                vout[ch, t, rows8(k + 1), :] = (1.0 - omega) * here[t] + omega * new
-        return carry
-
-    lax.fori_loop(0, K, body, 0, unroll=2)
+def fine_sweep(vin, vout, sp, wt, sl, omega):
+    def emit(k, ch, t, here, total):
+        new = sp[ch, t, rows8(k), :] + total
+        vout[ch, t, rows8(k + 1), :] = (1.0 - omega) * here + omega * new
+
+    stencil_pass(vin, wt, sl, emit)
     fine_pads(vout)
 
 
@@ -183,14 +202,14 @@
     fine_pads(vout)
 
 
-def fine_smooth(va, vb, sp, wt, from_zero):
+def fine_smooth(va, vb, sp, wt, sl, from_zero):
     bufs = [va, vb]
     at = 0
     for i in range(SWEEPS):
         if i == 0 and from_zero:
             fine_first(va, sp)
             continue
-        fine_sweep(bufs[at], bufs[1 - at], sp, wt, chebyshev_weight(i))
+        fine_sweep(bufs[at], bufs[1 - at], sp, wt, sl, chebyshev_weight(i))
         at = 1 - at
     return bufs[at], bufs[1 - at]
 
@@ -204,25 +223,20 @@
     return jnp.where(lane < 32, got[0], jnp.where(lane < 64, got[1], got[2]))
 
 
-def fine_residual_to_level(v, sp, wt, dg, lsrc):
+def fine_residual_to_level(v, sp, wt, dg, sl, lsrc):
     lane = lane_iota()
     idx = (4 * lane) % 128
-
-    def body(kl, carry):
-        acc = [[None] * 3 for _ in range(3)]
-        for q in range(4):
-            k = kl * 4 + q
-            w = fine_weights_at(wt, k)
-            for ch in range(3):
-                here, total = fine_neighbours(v, w, k, lane, ch)
-                for t in range(3):
-                    res = dg[t, rows8(k), :] * (sp[ch, t, rows8(k), :] - here[t] + total[t])
-                    acc[ch][t] = res if q == 0 else acc[ch][t] + res
-        for ch in range(3):
-            lsrc[ch, rows8(kl), :] = to_level(acc[ch], lane, idx) * 0.0625
-        return carry
-
-    lax.fori_loop(0, KL, body, 0)
+    acc = {}
+
+    def emit(k, ch, t, here, total):
+        res = dg[t, rows8(k), :] * (sp[ch, t, rows8(k), :] - here + total)
+        acc[ch, t] = acc[ch, t] + res if (ch, t) in acc else res
+
+    def end(m):
+        for ch in range(3):
+            lsrc[ch, rows8(m), :] = to_level([acc[ch, t] for t in range(3)], lane, idx) * 0.0625
+
+    stencil_pass(v, wt, sl, emit, begin=acc.clear, end=end)
 
 
 def level_weights(fx, fy, lw, ld, li, where):
@@ -429,34 +443,29 @@
     return fine, level
 
 
-def start_kernel(
-    n_row, n_col,
-    src, codes, labels, srows, crows, lrows, cols, corners,
-    sp, wt, dg, v, vpr, vpl, lev, lpr, lpl, g,
-    nat, fxp, fyp, va, vb, lsrc, lfx, lfy, lw, ld, li, lsp, fa, fb, lnat,
-):
-    where, lwhere = positions(n_row, n_col)
+TOP, LOW = pl.ds(0, HALO), pl.ds(ROWS - HALO, HALO)
+LTOP, LLOW = pl.ds(0, LHALO), pl.ds(LROWS - LHALO, LHALO)
+MID = pl.ds(8 + PAD, ROWS)
+ABOVE, BELOW = pl.ds(8 + PAD - HALO, HALO), pl.ds(8 + PAD + ROWS, HALO)
+
+
+class Sender:
+    def __init__(self, send_sems, recv_sems):
+        self.send_sems, self.recv_sems, self.count = send_sems, recv_sems, 0
+
+    def __call__(self, src, dst, device):
+        n = self.count
+        self.count += 1
+        copy = pltpu.make_async_remote_copy(
+            src_ref=src, dst_ref=dst, send_sem=self.send_sems.at[n], recv_sem=self.recv_sems.at[n],
+            device_id=device, device_id_type=MESH,
+        )
+        copy.start()
+        return copy
+
+
+def fine_operator(nat, fxp, fyp, sp, wt, dg, lfx, lfy, lnat, where):
     lane, sub = lane_iota(), sub_iota()
-    zero_ends(nat, 6)
-    mid, top, low = (
-        pl.ds(8 + PAD, ROWS),
-        pl.ds(8 + PAD - HALO, HALO),
-        pl.ds(8 + PAD + ROWS, HALO),
-    )
-    for t in range(2):
-        c = slice(128 * t, 128 * t + 128)
-        for a in range(3):
-            nat[a, t, mid, :] = src[a, :, c]
-            nat[a, t, top, :] = srows[0, a, :, c]
-            nat[a, t, low, :] = srows[1, a, :, c]
-        for a in range(2):
-            nat[3 + a, t, mid, :] = codes[a, :, c].astype(F32)
-            nat[3 + a, t, top, :] = crows[0, a, :, c].astype(F32)
-            nat[3 + a, t, low, :] = crows[1, a, :, c].astype(F32)
-        nat[5, t, mid, :] = labels[:, c].astype(F32)
-        nat[5, t, top, :] = lrows[0, :, c].astype(F32)
-        nat[5, t, low, :] = lrows[1, :, c].astype(F32)
-    unpack_columns(nat, 6, cols, corners, lane)
 
     def edge(code, a, b):
         return jnp.exp2(code * 0.25 - 2.0) * jnp.where(a != b, SEAM, 1.0)
@@ -474,7 +483,7 @@
             fyp[t, rows8(k), :] = jnp.where((row >= 1) & (row < where[2]), inner, 1.0)
         return carry
 
-    lax.fori_loop(0, K, faces, 0)
+    lax.fori_loop(0, K, faces, 0, unroll=2)
     for t in range(3):
         fyp[t, rows8(K), :] = pltpu.roll(fyp[t, rows8(0), :], 7, 0)
 
@@ -494,7 +503,7 @@
                 sp[ch, t, rows8(k), :] = nat[ch, t, at, :] * inv
         return carry
 
-    lax.fori_loop(0, K, weights, 0)
+    lax.fori_loop(0, K, weights, 0, unroll=2)
     idx = (4 * lane) % 128
 
     def level_faces(kl, carry):
@@ -511,161 +520,28 @@
         return carry
 
     lax.fori_loop(0, KL, level_faces, 0)
-    level_weights(lfx, lfy, lw, ld, li, lwhere)
-    field, _ = fine_smooth(va, vb, sp, wt, True)
-    fine_residual_to_level(field, sp, wt, dg, lsrc)
-    level_down(lsrc, li, ld, lw, lsp, fa, fb, lnat, lev, lpr, lpl, g)
-    field_out(field, nat, v, vpr, vpl)
-
-
-def cycle_kernel(
-    n_row, n_col,
-    sp, wt, dg, v_in, vrows, vcols, vcorn, lev_in, lrows, lcols, lcorn, corr,
-    v, vpr, vpl, lev, lpr, lpl, g,
-    nat, va, vb, lsrc, lfx, lfy, lw, ld, li, lsp, fa, fb, lnat, lnc,
+
+
+def coarse_solve(
+    n_row, n_col, place, send, g, s_cols, s_ext, t_back, row_eig, col_eig, v, vpr, vpl, lev, lpr, lpl,
+    vrows, vcols, vcorn, lrows, lcols, lcorn, one, two, three, mine, spec, back, corr,
 ):
-    where, lwhere = positions(n_row, n_col)
-    level = level_up(
-        lev_in, lrows, lcols, lcorn, corr, lnat, lnc, lfx, lfy, lw, ld, li, lsp, fa, fb, lwhere
-    )
-    fine_up(v_in, vrows, vcols, vcorn, level, nat, va, where)
-    field, other = fine_smooth(va, vb, sp, wt, False)
-    field, other = fine_smooth(field, other, sp, wt, False)
-    fine_residual_to_level(field, sp, wt, dg, lsrc)
-    level_down(lsrc, li, ld, lw, lsp, fa, fb, lnat, lev, lpr, lpl, g)
-    field_out(field, nat, v, vpr, vpl)
-
-
-def end_kernel(
-    n_row, n_col,
-    sp, wt, dg, v_in, vrows, vcols, vcorn, lev_in, lrows, lcols, lcorn, corr,
-    solution_out, residual_out,
-    nat, va, vb, lfx, lfy, lw, ld, li, lsp, fa, fb, lnat, lnc,
-):
-    where, lwhere = positions(n_row, n_col)
+    i, j, up, down, left, right = place
+    n_modes = n_row * CROWS
     lane = lane_iota()
-    level = level_up(
-        lev_in, lrows, lcols, lcorn, corr, lnat, lnc, lfx, lfy, lw, ld, li, lsp, fa, fb, lwhere
-    )
-    fine_up(v_in, vrows, vcols, vcorn, level, nat, va, where)
-    field, _ = fine_smooth(va, vb, sp, wt, False)
-
-    def body(k, carry):
-        at = pl.ds(8 + k, 8, stride=K)
-        w = fine_weights_at(wt, k)
-        for ch in range(3):
-            here, total = fine_neighbours(field, w, k, lane, ch)
-            for t in range(2):
-                nat[ch, t, at, :] = here[t]
-                res = dg[t, rows8(k), :] * (sp[ch, t, rows8(k), :] - here[t] + total[t])
-                nat[3 + ch, t, at, :] = res
-        return carry
-
-    lax.fori_loop(0, K, body, 0)
-    for ch in range(3):
-        for t in range(2):
-            c = slice(128 * t, 128 * t + 128)
-            solution_out[ch, :, c] = nat[ch, t, 8 + PAD : 8 + PAD + ROWS, :]
-            residual_out[ch, :, c] = nat[3 + ch, t, 8 + PAD : 8 + PAD + ROWS, :]
-
-
-def around(n_row, n_col):
-    i, j = lax.axis_index("row"), lax.axis_index("col")
-    up, down = lax.rem(i + n_row - 1, n_row), lax.rem(i + 1, n_row)
-    left, right = lax.rem(j + n_col - 1, n_col), lax.rem(j + 1, n_col)
-    return i, j, up, down, left, right
-
-
-def send(copies, src, dst, sems, device):
-    n = len(copies)
-    copy = pltpu.make_async_remote_copy(
-        src_ref=src, dst_ref=dst, send_sem=sems[0].at[n], recv_sem=sems[1].at[n],
-        device_id=device, device_id_type=MESH,
-    )
-    copy.start()
-    copies.append(copy)
-    return copy
-
-
-def exchange_kernel(
-    n_row, n_col,
-    src, codes, labels, src_v, codes_v, labels_v,
-    srows, crows, lrows, cols, corners,
-    right_pack, left_pack, send_sems, recv_sems,
-):
-    i, j, up, down, left, right = around(n_row, n_col)
-    barrier = pltpu.get_barrier_semaphore()
-    for r in (up, i, down):
-        for c in (left, j, right):
-            if r is not i or c is not j:
-                pl.semaphore_signal(barrier, inc=1, device_id=(r, c), device_id_type=MESH)
-    lane = lane_iota()
-
-    def tile_of(a, t, r):
-        c = slice(128 * t, 128 * t + 128)
-        if a < 3:
-            return src_v[a, r, c]
-        if a < 5:
-            return codes_v[a - 3, r, c].astype(F32)
-        return labels_v[r, c].astype(F32)
-
-    pack_fine(tile_of, 6, right_pack, left_pack, lane, ROWS)
-    pl.semaphore_wait(barrier, 8)
-    copies, sems = [], (send_sems, recv_sems)
-    top, low = pl.ds(0, HALO), pl.ds(ROWS - HALO, HALO)
-    send(copies, right_pack, cols.at[0], sems, (i, right))
-    send(copies, left_pack, cols.at[1], sems, (i, left))
-    for slot, rows, device in ((1, top, up), (0, low, down)):
-        send(copies, src.at[:, rows, :], srows.at[slot], sems, (device, j))
-        send(copies, codes.at[:, rows, :], crows.at[slot], sems, (device, j))
-        send(copies, labels.at[rows, :], lrows.at[slot], sems, (device, j))
-    send(copies, right_pack.at[:, low, :], corners.at[0], sems, (down, right))
-    send(copies, left_pack.at[:, low, :], corners.at[1], sems, (down, left))
-    send(copies, right_pack.at[:, top, :], corners.at[2], sems, (up, right))
-    send(copies, left_pack.at[:, top, :], corners.at[3], sems, (up, left))
-    for copy in copies:
-        copy.wait()
-
-
-def coarse_kernel(
-    n_row, n_col,
-    g, s_cols, s_rows, t_back, row_eig, col_eig, s_ext, v, vpr, vpl, lev, lpr, lpl,
-    vrows, vcols, vcorn, lrows, lcols, lcorn, corr,
-    one, two, three, mine, spec, back, send_sems, recv_sems,
-):
-    i, j, up, down, left, right = around(n_row, n_col)
-    n_modes = n_row * CROWS
-    barrier = pltpu.get_barrier_semaphore()
-    for d in range(1, n_col):
-        pl.semaphore_signal(barrier, inc=1, device_id=(i, lax.rem(j + d, n_col)), device_id_type=MESH)
-    for d in range(1, n_row):
-        pl.semaphore_signal(barrier, inc=1, device_id=(lax.rem(i + d, n_row), j), device_id_type=MESH)
-    for r in (up, down):
-        for c in (left, right):
-            pl.semaphore_signal(barrier, inc=1, device_id=(r, c), device_id_type=MESH)
-    pl.semaphore_wait(barrier, n_col + n_row + 2)
-    copies, sems = [], (send_sems, recv_sems)
-    lane = lane_iota()
-
-    first = [
-        send(copies, g, one.at[j], sems, (i, lax.rem(j + d, n_col))) for d in range(1, n_col)
+
+    first = [send(g, one.at[j], (i, lax.rem(j + d, n_col))) for d in range(1, n_col)]
+    one[j] = g[...]
+    halos = [
+        send(lpr, lcols.at[0], (i, right)),
+        send(lpl, lcols.at[1], (i, left)),
+        send(lev.at[:, LTOP, :], lrows.at[1], (up, j)),
+        send(lev.at[:, LLOW, :], lrows.at[0], (down, j)),
+        send(lpr.at[LLOW, :], lcorn.at[0], (down, right)),
+        send(lpl.at[LLOW, :], lcorn.at[1], (down, left)),
+        send(lpr.at[LTOP, :], lcorn.at[2], (up, right)),
+        send(lpl.at[LTOP, :], lcorn.at[3], (up, left)),
     ]
-    one[j] = g[...]
-    halos = []
-    top, low = pl.ds(0, HALO), pl.ds(ROWS - HALO, HALO)
-    ltop, llow = pl.ds(0, LHALO), pl.ds(LROWS - LHALO, LHALO)
-
-    def halo(*args):
-        halos.append(send(copies, *args[:2], sems, args[2]))
-
-    halo(lpr, lcols.at[0], (i, right))
-    halo(lpl, lcols.at[1], (i, left))
-    halo(lev.at[:, ltop, :], lrows.at[1], (up, j))
-    halo(lev.at[:, llow, :], lrows.at[0], (down, j))
-    halo(lpr.at[llow, :], lcorn.at[0], (down, right))
-    halo(lpl.at[llow, :], lcorn.at[1], (down, left))
-    halo(lpr.at[ltop, :], lcorn.at[2], (up, right))
-    halo(lpl.at[ltop, :], lcorn.at[3], (up, left))
     for copy in first:
         copy.wait()
 
@@ -690,29 +566,29 @@
         total = total + pltpu.roll(lax.slice_in_dim(x, CROWS * ch, CROWS * ch + CROWS), CCOLS * ch, 1)
     mine[...] = total
     own = pl.ds(pl.multiple_of(i * CROWS, CROWS), CROWS)
-    second = [
-        send(copies, mine, two.at[own, :], sems, (lax.rem(i + d, n_row), j)) for d in range(1, n_row)
+    second = [send(mine, two.at[own, :], (lax.rem(i + d, n_row), j)) for d in range(1, n_row)]
+    two[own, :] = total
+    halos += [
+        send(vpr, vcols.at[0], (i, right)),
+        send(vpl, vcols.at[1], (i, left)),
+        send(vpr.at[:, LOW, :], vcorn.at[0], (down, right)),
+        send(vpl.at[:, LOW, :], vcorn.at[1], (down, left)),
+        send(vpr.at[:, TOP, :], vcorn.at[2], (up, right)),
+        send(vpl.at[:, TOP, :], vcorn.at[3], (up, left)),
     ]
-    two[own, :] = total
-    halo(vpr, vcols.at[0], (i, right))
-    halo(vpl, vcols.at[1], (i, left))
-    halo(vpr.at[:, low, :], vcorn.at[0], (down, right))
-    halo(vpl.at[:, low, :], vcorn.at[1], (down, left))
-    halo(vpr.at[:, top, :], vcorn.at[2], (up, right))
-    halo(vpl.at[:, top, :], vcorn.at[3], (up, left))
     for copy in second:
         copy.wait()
-    halo(v.at[:, :, top, :], vrows.at[1], (up, j))
-    halo(v.at[:, :, low, :], vrows.at[0], (down, j))
-    y = jnp.dot(s_rows[...], two[...], precision=HIGHEST, preferred_element_type=F32)
+    halos += [
+        send(v.at[:, :, TOP, :], vrows.at[1], (up, j)),
+        send(v.at[:, :, LOW, :], vrows.at[0], (down, j)),
+    ]
+    y = jnp.dot(s_ext[8 : 8 + n_modes, :], two[...], precision=HIGHEST, preferred_element_type=F32)
     eig = SCREEN + COARSE_SCALE * (row_eig[...] + col_eig[pl.ds(j, 1), :])
     spec[...] = y / eig
     rows = s_ext[pl.ds(pl.multiple_of(i * CROWS, CROWS), BROWS), :]
     z = jnp.dot(rows, spec[...], precision=HIGHEST, preferred_element_type=F32)
     back[...] = z
-    third = [
-        send(copies, back, three.at[j], sems, (i, lax.rem(j + d, n_col))) for d in range(1, n_col)
-    ]
+    third = [send(back, three.at[j], (i, lax.rem(j + d, n_col))) for d in range(1, n_col)]
     three[j] = z
     for copy in third:
         copy.wait()
@@ -721,6 +597,121 @@
     for ch in range(3):
         corr[ch] = lax.slice_in_dim(z, BROWS * ch, BROWS * ch + BROWS)
     for copy in halos:
+        copy.wait()
+
+
+def kernel(n_row, n_col, src, codes, labels, *refs):
+    s_cols, s_ext, t_back, row_eig, col_eig, solution_out, residual_out = refs[:7]
+    (
+        codes_v, labels_v, right_pack, left_pack, srows, crows, labrows, cols, corners,
+        nat, fxp, fyp, sp, wt, dg, va, vb, sl, v, vpr, vpl,
+        lsrc, lfx, lfy, lw, ld, li, lsp, fa, fb, lnat, lnc, lev, lpr, lpl, g,
+        one, two, three, mine, spec, back, corr,
+        vrows, vcols, vcorn, lrows, lcols, lcorn,
+        copy_sems, send_sems, recv_sems,
+    ) = refs[7:]
+    i, j = lax.axis_index("row"), lax.axis_index("col")
+    up, down = lax.rem(i + n_row - 1, n_row), lax.rem(i + 1, n_row)
+    left, right = lax.rem(j + n_col - 1, n_col), lax.rem(j + 1, n_col)
+    where, lwhere = positions(n_row, n_col)
+    lane = lane_iota()
+
+    barrier = pltpu.get_barrier_semaphore()
+    peers = [(i, lax.rem(j + d, n_col)) for d in range(1, n_col)]
+    peers += [(lax.rem(i + d, n_row), j) for d in range(1, n_row)]
+    peers += [(r, c) for r in (up, down) for c in (left, right)]
+    for peer in peers:
+        pl.semaphore_signal(barrier, inc=1, device_id=peer, device_id_type=MESH)
+
+    loads = [pltpu.make_async_copy(codes, codes_v, copy_sems.at[0])]
+    loads.append(pltpu.make_async_copy(labels, labels_v, copy_sems.at[1]))
+    for a in range(3):
+        for t in range(2):
+            part = src.at[a, :, pl.ds(128 * t, 128)]
+            loads.append(pltpu.make_async_copy(part, nat.at[a, t, MID, :], copy_sems.at[len(loads)]))
+    for copy in loads:
+        copy.start()
+    zero_ends(nat, 6)
+    for copy in loads:
+        copy.wait()
+
+    def convert(n, carry):
+        r = rows8(n)
+        at = pl.ds(pl.multiple_of(8 + PAD + 8 * n, 8), 8)
+        for t in range(2):
+            c = slice(128 * t, 128 * t + 128)
+            nat[3, t, at, :] = codes_v[0, r, c].astype(F32)
+            nat[4, t, at, :] = codes_v[1, r, c].astype(F32)
+            nat[5, t, at, :] = labels_v[r, c].astype(F32)
+        return carry
+
+    lax.fori_loop(0, ROWS // 8, convert, 0, unroll=2)
+
+    def natural(a, t, r):
+        return nat[a, t, pl.ds(pl.multiple_of(8 + PAD + r.start, 8), 8), :]
+
+    pack_fine(natural, 6, right_pack, left_pack, lane, ROWS)
+    pl.semaphore_wait(barrier, n_col + n_row + 2)
+    send = Sender(send_sems, recv_sems)
+    copies = [
+        send(right_pack, cols.at[0], (i, right)),
+        send(left_pack, cols.at[1], (i, left)),
+    ]
+    for slot, rows, device in ((1, TOP, up), (0, LOW, down)):
+        copies.append(send(src.at[:, rows, :], srows.at[slot], (device, j)))
+        copies.append(send(codes.at[:, rows, :], crows.at[slot], (device, j)))
+        copies.append(send(labels.at[rows, :], labrows.at[slot], (device, j)))
+    copies.append(send(right_pack.at[:, LOW, :], corners.at[0], (down, right)))
+    copies.append(send(left_pack.at[:, LOW, :], corners.at[1], (down, left)))
+    copies.append(send(right_pack.at[:, TOP, :], corners.at[2], (up, right)))
+    copies.append(send(left_pack.at[:, TOP, :], corners.at[3], (up, left)))
+    for copy in copies:
+        copy.wait()
+
+    for t in range(2):
+        c = slice(128 * t, 128 * t + 128)
+        for slot, rows in ((0, ABOVE), (1, BELOW)):
+            for a in range(3):
+                nat[a, t, rows, :] = srows[slot, a, :, c]
+            for a in range(2):
+                nat[3 + a, t, rows, :] = crows[slot, a, :, c].astype(F32)
+            nat[5, t, rows, :] = labrows[slot, :, c].astype(F32)
+    unpack_columns(nat, 6, cols, corners, lane)
+    fine_operator(nat, fxp, fyp, sp, wt, dg, lfx, lfy, lnat, where)
+    level_weights(lfx, lfy, lw, ld, li, lwhere)
+
+    field, other = fine_smooth(va, vb, sp, wt, sl, True)
+    for cycle in range(2):
+        fine_residual_to_level(field, sp, wt, dg, sl, lsrc)
+        level_down(lsrc, li, ld, lw, lsp, fa, fb, lnat, lev, lpr, lpl, g)
+        field_out(field, nat, v, vpr, vpl)
+        got = [ref.at[cycle] for ref in (vrows, vcols, vcorn, lrows, lcols, lcorn, one, two, three)]
+        coarse_solve(
+            n_row, n_col, (i, j, up, down, left, right), send, g, s_cols, s_ext, t_back, row_eig, col_eig,
+            v, vpr, vpl, lev, lpr, lpl, *got, mine, spec, back, corr,
+        )
+        level = level_up(
+            lev, got[3], got[4], got[5], corr, lnat, lnc, lfx, lfy, lw, ld, li, lsp, fa, fb, lwhere
+        )
+        fine_up(v, got[0], got[1], got[2], level, nat, va, where)
+        field, other = fine_smooth(va, vb, sp, wt, sl, False)
+        if cycle == 0:
+            field, other = fine_smooth(field, other, sp, wt, sl, False)
+
+    def emit(k, ch, t, here, total):
+        at = pl.ds(8 + k, 8, stride=K)
+        nat[ch, t, at, :] = here
+        nat[3 + ch, t, at, :] = dg[t, rows8(k), :] * (sp[ch, t, rows8(k), :] - here + total)
+
+    stencil_pass(field, wt, sl, emit, tiles=2)
+    stores = []
+    for a in range(6):
+        for t in range(2):
+            out = (solution_out if a < 3 else residual_out).at[a % 3, :, pl.ds(128 * t, 128)]
+            stores.append(pltpu.make_async_copy(nat.at[a, t, MID, :], out, copy_sems.at[len(stores)]))
+    for copy in stores:
+        copy.start()
+    for copy in stores:
         copy.wait()
 
 
@@ -749,7 +740,7 @@
     s_ext = np.zeros((nr + 16, nr))
     s_ext[8 : 8 + nr] = rows
     row_eig = np.repeat(eig(nr)[:, None], 128, axis=1)
-    return tuple(x.astype(np.float32) for x in (s_cols, rows, t_back, row_eig, col_eig, s_ext))
+    return tuple(x.astype(np.float32) for x in (s_cols, s_ext, t_back, row_eig, col_eig))
 
 
 def shape(*dims, dtype=F32):
@@ -762,80 +753,44 @@
 
 def solution(mesh):
     n_row, n_col = mesh.shape["row"], mesh.shape["col"]
-    fine = functools.partial(pltpu.VMEM, dtype=F32)
-    params = pltpu.CompilerParams(vmem_limit_bytes=VMEM_LIMIT)
-
-    def level_scratch():
-        flat = pltpu.VMEM((KL * 8, 128), F32)
-        padded = pltpu.VMEM((3, (KL + 2) * 8, 128), F32)
-        return [
-            flat, pltpu.VMEM(((KL + 1) * 8, 128), F32), pltpu.VMEM((4, KL * 8, 128), F32), flat, flat,
-            pltpu.VMEM((3, KL * 8, 128), F32), padded, padded, pltpu.VMEM((11, LNAT, 128), F32),
-        ]
-
-    padded = pltpu.VMEM((3, 3, (K + 2) * 8, 128), F32)
-    lsrc = pltpu.VMEM((3, KL * 8, 128), F32)
-    lnc = pltpu.VMEM((3, LNAT, 128), F32)
-    nat = lambda n: pltpu.VMEM((n, 3, NAT, 128), F32)
-    down_shapes = [
-        shape(3, 2, ROWS, 128), shape(1, ROWS, 128), shape(1, ROWS, 128), shape(8, LROWS, 128),
-        shape(LROWS, 128), shape(LROWS, 128), shape(CROWS, 128),
+
+    def vmem(*dims, dtype=F32):
+        return pltpu.VMEM(dims, dtype)
+
+    n_copies = 12 + 2 * (2 * (n_col - 1) + (n_row - 1) + 16)
+    scratch = [
+        vmem(2, ROWS, COLS, dtype=jnp.int32), vmem(ROWS, COLS, dtype=jnp.int32),
+        vmem(2, ROWS, 128), vmem(2, ROWS, 128),
+        vmem(2, 3, HALO, COLS), vmem(2, 2, HALO, COLS, dtype=jnp.int32), vmem(2, HALO, COLS, dtype=jnp.int32),
+        vmem(2, 2, ROWS, 128), vmem(4, 2, HALO, 128),
+        vmem(6, 3, NAT, 128), vmem(3, K * 8, 128), vmem(3, (K + 1) * 8, 128),
+        vmem(3, 3, K * 8, 128), vmem(4, 3, K * 8, 128), vmem(3, K * 8, 128),
+        vmem(3, 3, (K + 4) * 8, 128), vmem(3, 3, (K + 4) * 8, 128), vmem(4, 2, 3, 3, 8, 128),
+        vmem(3, 2, ROWS, 128), vmem(1, ROWS, 128), vmem(1, ROWS, 128),
+        vmem(3, KL * 8, 128), vmem(KL * 8, 128), vmem((KL + 1) * 8, 128),
+        vmem(4, KL * 8, 128), vmem(KL * 8, 128), vmem(KL * 8, 128), vmem(3, KL * 8, 128),
+        vmem(3, (KL + 2) * 8, 128), vmem(3, (KL + 2) * 8, 128),
+        vmem(11, LNAT, 128), vmem(3, LNAT, 128), vmem(8, LROWS, 128),
+        vmem(LROWS, 128), vmem(LROWS, 128), vmem(CROWS, 128),
+        vmem(2, n_col, CROWS, 128), vmem(2, n_row * CROWS, 128), vmem(2, n_col, BROWS, 128),
+        vmem(CROWS, 128), vmem(n_row * CROWS, 128), vmem(BROWS, 128), vmem(3, BROWS, 128),
+        vmem(2, 2, 3, 2, HALO, 128), vmem(2, 2, 1, ROWS, 128), vmem(2, 4, 1, HALO, 128),
+        vmem(2, 2, 8, LHALO, 128), vmem(2, 2, LROWS, 128), vmem(2, 4, LHALO, 128),
+        pltpu.SemaphoreType.DMA((12,)),
+        pltpu.SemaphoreType.DMA((n_copies,)), pltpu.SemaphoreType.DMA((n_copies,)),
     ]
-    n_coarse = 2 * (n_col - 1) + (n_row - 1) + 16
-
-    def call(kernel, n_in, outs, scratch):
-        return pl.pallas_call(
-            functools.partial(kernel, n_row, n_col), out_shape=outs, in_specs=[IN_VMEM] * n_in,
-            out_specs=[IN_VMEM] * len(outs), scratch_shapes=scratch, compiler_params=params,
-        )
-
-    exchange = pl.pallas_call(
-        functools.partial(exchange_kernel, n_row, n_col),
-        out_shape=[
-            shape(2, 3, HALO, COLS), shape(2, 2, HALO, COLS, dtype=jnp.int32), shape(2, HALO, COLS, dtype=jnp.int32),
-            shape(2, 2, ROWS, 128), shape(4, 2, HALO, 128),
-        ],
-        in_specs=[IN_ANY] * 3 + [IN_VMEM] * 3,
-        out_specs=[IN_VMEM] * 5,
-        scratch_shapes=[pltpu.VMEM((2, ROWS, 128), F32)] * 2 + [pltpu.SemaphoreType.DMA((12,))] * 2,
+    call = pl.pallas_call(
+        functools.partial(kernel, n_row, n_col),
+        out_shape=[shape(3, ROWS, COLS)] * 2,
+        in_specs=[IN_ANY] * 3 + [IN_VMEM] * 5,
+        out_specs=[IN_ANY] * 2,
+        scratch_shapes=scratch,
         compiler_params=pltpu.CompilerParams(collective_id=0, has_side_effects=True, vmem_limit_bytes=VMEM_LIMIT),
     )
-    start = call(
-        start_kernel, 8,
-        [shape(3, 3, K * 8, 128), shape(4, 3, K * 8, 128), shape(3, K * 8, 128)] + down_shapes,
-        [nat(6), pltpu.VMEM((3, K * 8, 128), F32), pltpu.VMEM((3, (K + 1) * 8, 128), F32), padded, padded, lsrc]
-        + level_scratch(),
-    )
-    coarse = pl.pallas_call(
-        functools.partial(coarse_kernel, n_row, n_col),
-        out_shape=[
-            shape(2, 3, 2, HALO, 128), shape(2, 1, ROWS, 128), shape(4, 1, HALO, 128),
-            shape(2, 8, LHALO, 128), shape(2, LROWS, 128), shape(4, LHALO, 128), shape(3, BROWS, 128),
-        ],
-        in_specs=[IN_VMEM] * 7 + [IN_ANY] * 6,
-        out_specs=[IN_VMEM] * 7,
-        scratch_shapes=[
-            pltpu.VMEM((n_col, CROWS, 128), F32), pltpu.VMEM((n_row * CROWS, 128), F32),
-            pltpu.VMEM((n_col, BROWS, 128), F32), pltpu.VMEM((CROWS, 128), F32),
-            pltpu.VMEM((n_row * CROWS, 128), F32), pltpu.VMEM((BROWS, 128), F32),
-            pltpu.SemaphoreType.DMA((n_coarse,)), pltpu.SemaphoreType.DMA((n_coarse,)),
-        ],
-        compiler_params=pltpu.CompilerParams(collective_id=1, has_side_effects=True, vmem_limit_bytes=VMEM_LIMIT),
-    )
-    cycle = call(cycle_kernel, 12, down_shapes, [nat(3), padded, padded, lsrc] + level_scratch() + [lnc])
-    end = call(
-        end_kernel, 12, [shape(3, ROWS, COLS)] * 2, [nat(6), padded, padded] + level_scratch() + [lnc]
-    )
     consts = tables(n_row, n_col)
 
     def local(sources, edge_codes, seam_labels):
-        halos = exchange(sources, edge_codes, seam_labels, sources, edge_codes, seam_labels)
-        sp, wt, dg, *down = start(sources, edge_codes, seam_labels, *halos)
-        for step in (cycle, end):
-            v, vpr, vpl, lev, lpr, lpl, g = down
-            vrows, vcols, vcorn, lrows, lcols, lcorn, corr = coarse(g, *consts, v, vpr, vpl, lev, lpr, lpl)
-            down = step(sp, wt, dg, v, vrows, vcols, vcorn, lev, lrows, lcols, lcorn, corr)
-        return tuple(down)
+        return tuple(call(sources, edge_codes, seam_labels, *consts))
 
     spec = P(None, "row", "col")
     return jax.shard_map(

time: 263 us -> 208 us (0.79)
  Pallas kernels: 263 us -> 203 us
  local copies, waits for them, and re-layouts: 0 us -> 3.92 us
    pallas_call x6 -> x1, Pallas kernels: 263 us -> 203 us  [local(): return tuple(call(sources, edge_codes, seam_labels, *consts))]
    unnamed x0 -> x4, local copies, waits for them, and re-layouts: none -> 3.92 us
where the time goes in v2:
time: 208 us; the launch traced here: 207 us
  Pallas kernels  203 us (98%)
  local copies, waits for them, and re-layouts  3.92 us (2%)
    pallas_call x1, Pallas kernels, local(): return tuple(call(sources, edge_codes, seam_labels, *consts))  203 us

profile of v2, /device:TPU:1, one launch (start us, length us, event | category | flops | bytes accessed | tf_op | source)
XLA Modules:
  0.0 207.5 jit_solution(1450429038587123154)
XLA Ops:
  0.6 202.9 %shard_map.95 = (f32[3,512,256]{2,1,0:T(8,128)}, f32[3,512,256]{2,1,0:T(8,128)}) custom-call(f32[3,512,256]{2,1,0:T(8,128)} %src.1, s32[2,512,256]{2,1,0:T(8,128)} %codes.1, s32[512,256]{1,0:T(8,128)} %labels.1, f32[8,128,128]{2,1,0:T(8,128)} %constant.10.clone.refs_0_, f32[528,512]{1,0:T(8,128)} %constant.11.clone.refs_1_, ...), custom_call_target="tpu_custom_call" | custom-call | tf_op jit(solution)/shard_map/pallas_call | solution.py:793
  203.5 0.0 copy-start
  203.6 2.8 %copy.12 = f32[3,512,256]{2,1,0:T(8,128)} copy(f32[3,512,256]{2,1,0:T(8,128)} %get-tuple-element.4) | data formatting | bytes 3145728
  206.3 0.0 copy-done
  206.3 1.1 copy.13
Async XLA Ops:
  203.5 2.8 %copy-start = (f32[3,512,256]{2,1,0:T(8,128)S(1)}, f32[3,512,256]{2,1,0:T(8,128)}, u32[]{:S(2)}) copy-start(f32[3,512,256]{2,1,0:T(8,128)} %get-tuple-element.5) | copy-start | bytes 4718596

commit v3 on v2

--- a/solution.py
+++ b/solution.py
@@ -62,11 +62,6 @@
     return [jnp.where(lane == 0, rolled[(t + 2) % 3], rolled[t]) for t in range(3)]
 
 
-def right_of(tiles, lane):
-    rolled = [lroll(x, 127) for x in tiles]
-    return [jnp.where(lane == 127, rolled[(t + 1) % 3], rolled[t]) for t in range(3)]
-
-
 def set_pads(ref, lead, count):
     last = ref[lead + (rows8(count), slice(None))]
     first = ref[lead + (rows8(1), slice(None))]
@@ -119,59 +114,107 @@
     unpack_fine(nat, n_arrays, 8 + PAD + ROWS, HALO // 8, corners.at[2], corners.at[3], lane)
 
 
+CPAD = 64
+EDGE, EDGE_RIGHT, EDGE_LEFT = 11, 96, 21
+
+
+def pack_field(nat, right, left):
+    lane = lane_iota()
+
+    def body(i, carry):
+        r = pl.ds(pl.multiple_of(8 + PAD + i * 8, 8), 8)
+        out_r = out_l = jnp.zeros((8, 128), F32)
+        for q in range(9):
+            x = nat[q // 3, q % 3, r, :]
+            here = (lane >= EDGE * q) & (lane < EDGE * q + EDGE)
+            out_r = jnp.where(here, lroll(x, EDGE * q - EDGE_RIGHT), out_r)
+            out_l = jnp.where(here, lroll(x, EDGE * q - EDGE_LEFT), out_l)
+        right[rows8(i), :] = out_r
+        left[rows8(i), :] = out_l
+        return carry
+
+    lax.fori_loop(0, ROWS // 8, body, 0, unroll=2)
+
+
+def unpack_field(nat, at, count, own, from_left, from_right):
+    lane = lane_iota()
+
+    def body(i, carry):
+        dst = pl.ds(pl.multiple_of(at + i * 8, 8), 8)
+        l, r = from_left[rows8(i), :], from_right[rows8(i), :]
+        for ch in range(3):
+            for t in range(3):
+                p = 3 * lane + t
+                u = (t + 1) % 3
+                a = lroll(l, EDGE_RIGHT - (86 if u == 0 else 85) - EDGE * (3 * ch + u))
+                u = (t + 2) % 3
+                b = lroll(r, EDGE_LEFT + (86 if u == 2 else 85) - EDGE * (3 * ch + u))
+                x = jnp.where((p >= CPAD - HALO) & (p < CPAD), a, own(ch, t, i, dst))
+                x = jnp.where((p >= CPAD + COLS) & (p < CPAD + COLS + HALO), b, x)
+                nat[ch, t, dst, :] = x
+        return carry
+
+    lax.fori_loop(0, count, body, 0)
+
+
+def dealt(x, lane):
+    out = []
+    for t in range(3):
+        p = 3 * lane + t
+        got = [lanes_take(y, (p - CPAD) % 128) for y in x]
+        out.append(jnp.where((p < 64) | (p >= 320), got[2], jnp.where(p < 192, got[0], got[1])))
+    return out
+
+
+def undealt(x, lane):
+    out = []
+    for t in range(2):
+        p = lane + (128 * t + CPAD)
+        got = [lanes_take(y, p // 3) for y in x]
+        out.append(jnp.where(p % 3 == 0, got[0], jnp.where(p % 3 == 1, got[1], got[2])))
+    return out
+
+
+def natural_place(k, t, lane, sub, row0, col0):
+    row = row0 - PAD + sub * K + k
+    if t < 2:
+        return row, lane + (col0 + 128 * t)
+    return row, jnp.where(lane < 64, lane + (col0 + 256), lane + (col0 - 128))
+
+
 def fine_inside(k, t, lane, sub, row0, col0, n_rows, n_cols):
     row = row0 - PAD + sub * K + k
-    if t < 2:
-        col = lane + (col0 + 128 * t)
-    else:
-        col = jnp.where(lane < 64, lane + (col0 + 256), lane + (col0 - 128))
-    return (row >= 0) & (row < n_rows) & (col >= 0) & (col < n_cols), row, col
+    col = 3 * lane + (t - CPAD + col0)
+    return (row >= 0) & (row < n_rows) & (col >= 0) & (col < n_cols)
 
 
 def level_inside(k, lane, sub, row0, col0, n_rows, n_cols):
     row = row0 - LPAD + sub * KL + k
-    col = jnp.where(lane < 96, lane, lane - 128) + col0
-    return (row >= 0) & (row < n_rows) & (col >= 0) & (col < n_cols)
-
-
-def stencil_pass(v, wt, sl, emit, tiles=3, begin=None, end=None):
-    lane = lane_iota()
-
-    def shift(k, slot):
+    col = lane - LHALO + col0
+    return (row >= 0) & (row < n_rows) & (col >= 0) & (col < n_cols) & (lane < 96)
+
+
+def stencil_pass(v, wt, emit, unroll, end=None):
+    def row(k):
+        w = [[wt[n, t, rows8(k), :] for t in range(3)] for n in range(4)]
         for ch in range(3):
             here = [v[ch, t, rows8(k + 1), :] for t in range(3)]
-            left, right = left_of(here, lane), right_of(here, lane)
+            left = [lroll(here[2], 1), here[0], here[1]]
+            right = [here[1], here[2], lroll(here[0], 127)]
+            total = []
             for t in range(3):
-                sl[slot, 0, ch, t] = left[t]
-                sl[slot, 1, ch, t] = right[t]
-
-    def compute(k, slot):
-        for t in range(tiles):
-            w = [wt[n, t, rows8(k), :] for n in range(4)]
-            for ch in range(3):
-                total = w[0] * sl[slot, 0, ch, t] + w[1] * sl[slot, 1, ch, t]
-                total = total + w[2] * v[ch, t, rows8(k), :] + w[3] * v[ch, t, rows8(k + 2), :]
-                emit(k, ch, t, v[ch, t, rows8(k + 1), :], total)
+                x = w[2][t] * v[ch, t, rows8(k), :] + w[3][t] * v[ch, t, rows8(k + 2), :]
+                total.append(x + (w[0][t] * left[t] + w[1][t] * right[t]))
+            emit(k, ch, here, total)
 
     def body(m, carry):
-        k = 4 * m
-        if begin is not None:
-            begin()
-        shift(k + 2, 2)
-        shift(k + 3, 3)
-        compute(k, 0)
-        compute(k + 1, 1)
-        shift(k + 4, 0)
-        shift(k + 5, 1)
-        compute(k + 2, 2)
-        compute(k + 3, 3)
+        for q in range(unroll):
+            row(unroll * m + q)
         if end is not None:
             end(m)
         return carry
 
-    shift(0, 0)
-    shift(1, 1)
-    lax.fori_loop(0, K // 4, body, 0)
+    lax.fori_loop(0, K // unroll, body, 0)
 
 
 def fine_pads(v):
@@ -180,12 +223,13 @@
             set_pads(v, (ch, t), K)
 
 
-def fine_sweep(vin, vout, sp, wt, sl, omega):
-    def emit(k, ch, t, here, total):
-        new = sp[ch, t, rows8(k), :] + total
-        vout[ch, t, rows8(k + 1), :] = (1.0 - omega) * here + omega * new
-
-    stencil_pass(vin, wt, sl, emit)
+def fine_sweep(vin, vout, sp, wt, omega):
+    def emit(k, ch, here, total):
+        for t in range(3):
+            new = sp[ch, t, rows8(k), :] + total[t]
+            vout[ch, t, rows8(k + 1), :] = (1.0 - omega) * here[t] + omega * new
+
+    stencil_pass(vin, wt, emit, 4)
     fine_pads(vout)
 
 
@@ -202,41 +246,43 @@
     fine_pads(vout)
 
 
-def fine_smooth(va, vb, sp, wt, sl, from_zero):
+def fine_smooth(va, vb, sp, wt, from_zero):
     bufs = [va, vb]
     at = 0
     for i in range(SWEEPS):
         if i == 0 and from_zero:
             fine_first(va, sp)
             continue
-        fine_sweep(bufs[at], bufs[1 - at], sp, wt, sl, chebyshev_weight(i))
+        fine_sweep(bufs[at], bufs[1 - at], sp, wt, chebyshev_weight(i))
         at = 1 - at
     return bufs[at], bufs[1 - at]
 
 
-def to_level(x, lane, idx):
-    got = []
-    for y in x:
-        y = y + lroll(y, 127)
-        y = y + lroll(y, 126)
-        got.append(lanes_take(y, idx))
-    return jnp.where(lane < 32, got[0], jnp.where(lane < 64, got[1], got[2]))
-
-
-def fine_residual_to_level(v, sp, wt, dg, sl, lsrc):
+def pick(x, lane):
+    got = [lanes_take(y, jnp.minimum((4 * lane) // 3, 127)) for y in x]
+    return jnp.where(lane % 3 == 0, got[0], jnp.where(lane % 3 == 1, got[1], got[2]))
+
+
+def to_level(x, lane):
+    after = [lroll(y, 127) for y in x]
+    mid, first = x[1] + x[2], after[0] + after[1]
+    sums = [x[0] + mid + after[0], mid + first, x[2] + first + after[2]]
+    return pick(sums, lane)
+
+
+def fine_residual_to_level(v, sp, wt, dg, lsrc):
     lane = lane_iota()
-    idx = (4 * lane) % 128
     acc = {}
 
-    def emit(k, ch, t, here, total):
-        res = dg[t, rows8(k), :] * (sp[ch, t, rows8(k), :] - here + total)
-        acc[ch, t] = acc[ch, t] + res if (ch, t) in acc else res
+    def emit(k, ch, here, total):
+        res = [dg[t, rows8(k), :] * (sp[ch, t, rows8(k), :] - here[t] + total[t]) for t in range(3)]
+        acc[ch] = [a + b for a, b in zip(acc[ch], res)] if ch in acc else res
 
     def end(m):
         for ch in range(3):
-            lsrc[ch, rows8(m), :] = to_level([acc[ch, t] for t in range(3)], lane, idx) * 0.0625
-
-    stencil_pass(v, wt, sl, emit, begin=acc.clear, end=end)
+            lsrc[ch, rows8(m), :] = to_level(acc.pop(ch), lane) * 0.0625
+
+    stencil_pass(v, wt, emit, 4, end)
 
 
 def level_weights(fx, fy, lw, ld, li, where):
@@ -281,7 +327,7 @@
                     src[ch, rows8(k + 1), :] = omega * lsp[ch, rows8(k), :]
                 return carry
 
-            lax.fori_loop(0, KL, first, 0)
+            lax.fori_loop(0, KL, first, 0, unroll=True)
             level_pads(src)
             continue
 
@@ -291,7 +337,7 @@
                 dst[ch, rows8(k + 1), :] = (1.0 - omega) * here + omega * (lsp[ch, rows8(k), :] + total)
             return carry
 
-        lax.fori_loop(0, KL, body, 0)
+        lax.fori_loop(0, KL, body, 0, unroll=True)
         level_pads(dst)
         at = 1 - at
     return bufs[at]
@@ -305,7 +351,7 @@
             lsp[ch, rows8(k), :] = lsrc[ch, rows8(k), :] * li[rows8(k), :]
         return carry
 
-    lax.fori_loop(0, KL, scale, 0)
+    lax.fori_loop(0, KL, scale, 0, unroll=True)
     f = level_smooth(fa, fb, lsp, lw, True)
 
     def out(k, carry):
@@ -317,7 +363,7 @@
             lnat[3 + ch, at, :] = lsrc[ch, rows8(k), :]
         return carry
 
-    lax.fori_loop(0, KL, out, 0)
+    lax.fori_loop(0, KL, out, 0, unroll=True)
 
     def copy(i, carry):
         src = pl.ds(pl.multiple_of(LHALO + i * 8, 8), 8)
@@ -326,14 +372,14 @@
             x = lnat[a, src, :]
             lev[a, rows8(i), :] = x
             here = (lane >= 16 * a) & (lane < 16 * a + 16)
-            right = jnp.where(here, lroll(x, 16 * a - 48), right)
-            left = jnp.where(here, lroll(x, 16 * a), left)
+            right = jnp.where(here, lroll(x, 16 * a - 64), right)
+            left = jnp.where(here, lroll(x, 16 * a - 16), left)
         lpr[rows8(i), :] = right
         lpl[rows8(i), :] = left
         return carry
 
     lax.fori_loop(0, LROWS // 8, copy, 0)
-    idx = (4 * lane) % 128
+    idx = (LHALO + 4 * lane) % 128
     for i in range(CROWS // 8):
         total = jnp.zeros((8, 128), F32)
         for ch in range(3):
@@ -353,9 +399,9 @@
             dst = pl.ds(pl.multiple_of(dst_row + i * 8, 8), 8)
             l, r = left(rows8(i)), right(rows8(i))
             for a in range(8):
-                x = jnp.where(lane < 64, own(a, rows8(i)), 0.0)
-                x = jnp.where((lane >= 64) & (lane < 80), lroll(r, 64 - 16 * a), x)
-                lnat[a, dst, :] = jnp.where(lane >= 112, lroll(l, 112 - 16 * a), x)
+                x = jnp.where((lane >= 80) & (lane < 96), lroll(r, 80 - 16 * a), 0.0)
+                x = jnp.where((lane >= 16) & (lane < 80), own(a, rows8(i)), x)
+                lnat[a, dst, :] = jnp.where(lane < 16, lroll(l, -16 * a), x)
             return carry
 
         lax.fori_loop(0, count, body, 0)
@@ -387,53 +433,44 @@
             lsp[ch, rows8(k), :] = lnat[3 + ch, at, :] * inv
         return carry
 
-    lax.fori_loop(0, KL, fields, 0)
+    lax.fori_loop(0, KL, fields, 0, unroll=True)
     level_pads(fa)
     return level_smooth(fa, fb, lsp, lw, False)
 
 
-def fine_up(v, vrows, vcols, vcorn, field, nat, va, where):
+def fine_up(vrows, vcols, vcorn, field, nat, va, where):
     lane, sub = lane_iota(), sub_iota()
-    zero_ends(nat, 3)
-    for ch in range(3):
-        for t in range(2):
-            nat[ch, t, 8 + PAD : 8 + PAD + ROWS, :] = v[ch, t]
-            nat[ch, t, 8 + PAD - HALO : 8 + PAD, :] = vrows[0, ch, t]
-            nat[ch, t, 8 + PAD + ROWS : 8 + PAD + ROWS + HALO, :] = vrows[1, ch, t]
-    unpack_columns(nat, 3, vcols, vcorn, lane)
-    quarter = lane // 4
-    idx = [quarter, 32 + quarter, jnp.where(lane < 64, 64 + quarter, 96 + quarter)]
+    unpack_field(nat, 8 + PAD, ROWS // 8, lambda ch, t, i, r: nat[ch, t, r, :], vcols.at[0], vcols.at[1])
+    for slot, at in ((0, 8 + PAD - HALO), (1, 8 + PAD + ROWS)):
+        own = lambda ch, t, i, r, slot=slot: vrows[slot, ch, t, rows8(i), :]
+        unpack_field(nat, at, HALO // 8, own, vcorn.at[2 * slot], vcorn.at[2 * slot + 1])
 
     def body(kl, carry):
-        for ch in range(3):
-            level = field[ch, rows8(kl + 1), :]
-            for t in range(3):
-                add = lanes_take(level, idx[t])
+        for t in range(3):
+            idx = jnp.minimum((3 * lane + t) // 4, 127)
+            inside = [fine_inside(kl * 4 + q, t, lane, sub, *where) for q in range(4)]
+            for ch in range(3):
+                add = lanes_take(field[ch, rows8(kl + 1), :], idx)
                 for q in range(4):
-                    k = kl * 4 + q
-                    inside = fine_inside(k, t, lane, sub, *where)[0]
-                    x = nat[ch, t, pl.ds(8 + k, 8, stride=K), :] + add
-                    va[ch, t, rows8(k + 1), :] = jnp.where(inside, x, 0.0)
+                    x = nat[ch, t, pl.ds(8 + kl * 4 + q, 8, stride=K), :] + add
+                    va[ch, t, rows8(kl * 4 + q + 1), :] = jnp.where(inside[q], x, 0.0)
         return carry
 
     lax.fori_loop(0, KL, body, 0)
     fine_pads(va)
 
 
-def field_out(field, nat, v, vpr, vpl):
-    lane = lane_iota()
-
-    def body(k, carry):
-        for ch in range(3):
-            for t in range(2):
-                nat[ch, t, pl.ds(8 + k, 8, stride=K), :] = field[ch, t, rows8(k + 1), :]
-        return carry
-
-    lax.fori_loop(0, K, body, 0)
-    for ch in range(3):
-        for t in range(2):
-            v[ch, t] = nat[ch, t, 8 + PAD : 8 + PAD + ROWS, :]
-    pack_fine(lambda a, t, r: v[a, t, r, :], 3, vpr, vpl, lane, ROWS)
+def field_out(field, nat, vpr, vpl):
+    def body(m, carry):
+        for q in range(2):
+            k = 2 * m + q
+            for ch in range(3):
+                for t in range(3):
+                    nat[ch, t, pl.ds(8 + k, 8, stride=K), :] = field[ch, t, rows8(k + 1), :]
+        return carry
+
+    lax.fori_loop(0, K // 2, body, 0)
+    pack_field(nat, vpr, vpl)
 
 
 def positions(n_row, n_col):
@@ -446,6 +483,7 @@
 TOP, LOW = pl.ds(0, HALO), pl.ds(ROWS - HALO, HALO)
 LTOP, LLOW = pl.ds(0, LHALO), pl.ds(LROWS - LHALO, LHALO)
 MID = pl.ds(8 + PAD, ROWS)
+FIRST, LAST = pl.ds(8 + PAD, HALO), pl.ds(8 + PAD + ROWS - HALO, HALO)
 ABOVE, BELOW = pl.ds(8 + PAD - HALO, HALO), pl.ds(8 + PAD + ROWS, HALO)
 
 
@@ -475,12 +513,17 @@
         code = left_of([nat[3, t, at, :] for t in range(3)], lane)
         label = [nat[5, t, at, :] for t in range(3)]
         beside = left_of(label, lane)
+        fx, fy = [], []
         for t in range(3):
-            _, row, col = fine_inside(k, t, lane, sub, *where)
+            row, col = natural_place(k, t, lane, sub, where[0], where[1])
             inner = edge(code[t], beside[t], label[t])
-            fxp[t, rows8(k), :] = jnp.where((col >= 1) & (col < where[3]), inner, 1.0)
+            fx.append(jnp.where((col >= 1) & (col < where[3]), inner, 1.0))
             inner = edge(nat[4, t, above, :], nat[5, t, above, :], label[t])
-            fyp[t, rows8(k), :] = jnp.where((row >= 1) & (row < where[2]), inner, 1.0)
+            fy.append(jnp.where((row >= 1) & (row < where[2]), inner, 1.0))
+        for t, x in enumerate(dealt(fx, lane)):
+            fxp[t, rows8(k), :] = x
+        for t, x in enumerate(dealt(fy, lane)):
+            fyp[t, rows8(k), :] = x
         return carry
 
     lax.fori_loop(0, K, faces, 0, unroll=2)
@@ -489,29 +532,28 @@
 
     def weights(k, carry):
         left = [fxp[t, rows8(k), :] for t in range(3)]
-        right = right_of(left, lane)
+        right = [left[1], left[2], lroll(left[0], 127)]
         at = pl.ds(8 + k, 8, stride=K)
+        scale = []
         for t in range(3):
             up, down = fyp[t, rows8(k), :], fyp[t, rows8(k + 1), :]
             diag = SCREEN + left[t] + right[t] + up + down
-            inside = fine_inside(k, t, lane, sub, *where)[0]
-            inv = jnp.where(inside, 1.0 / diag, 0.0)
+            inv = jnp.where(fine_inside(k, t, lane, sub, *where), 1.0 / diag, 0.0)
+            scale.append(inv)
             dg[t, rows8(k), :] = diag
             for n, face in enumerate((left[t], right[t], up, down)):
                 wt[n, t, rows8(k), :] = face * inv
-            for ch in range(3):
-                sp[ch, t, rows8(k), :] = nat[ch, t, at, :] * inv
+        for ch in range(3):
+            for t, x in enumerate(dealt([nat[ch, t, at, :] for t in range(3)], lane)):
+                sp[ch, t, rows8(k), :] = x * scale[t]
         return carry
 
     lax.fori_loop(0, K, weights, 0, unroll=2)
-    idx = (4 * lane) % 128
 
     def level_faces(kl, carry):
-        got = [
-            lanes_take(sum(fxp[t, rows8(kl * 4 + q), :] for q in range(4)), idx) for t in range(3)
-        ]
-        x = jnp.where(lane < 32, got[0], jnp.where(lane < 64, got[1], got[2])) * 0.0625
-        y = to_level([fyp[t, rows8(kl * 4), :] for t in range(3)], lane, idx) * 0.0625
+        rows = [sum(fxp[t, rows8(kl * 4 + q), :] for q in range(4)) for t in range(3)]
+        x = pick(rows, lane) * 0.0625
+        y = to_level([fyp[t, rows8(kl * 4), :] for t in range(3)], lane) * 0.0625
         at = pl.ds(LHALO - LPAD + kl, 8, stride=KL)
         lfx[rows8(kl), :] = x
         lfy[rows8(kl), :] = y
@@ -523,7 +565,7 @@
 
 
 def coarse_solve(
-    n_row, n_col, place, send, g, s_cols, s_ext, t_back, row_eig, col_eig, v, vpr, vpl, lev, lpr, lpl,
+    n_row, n_col, place, send, g, s_cols, s_ext, t_back, row_eig, col_eig, nat, vpr, vpl, lev, lpr, lpl,
     vrows, vcols, vcorn, lrows, lcols, lcorn, one, two, three, mine, spec, back, corr,
 ):
     i, j, up, down, left, right = place
@@ -571,16 +613,16 @@
     halos += [
         send(vpr, vcols.at[0], (i, right)),
         send(vpl, vcols.at[1], (i, left)),
-        send(vpr.at[:, LOW, :], vcorn.at[0], (down, right)),
-        send(vpl.at[:, LOW, :], vcorn.at[1], (down, left)),
-        send(vpr.at[:, TOP, :], vcorn.at[2], (up, right)),
-        send(vpl.at[:, TOP, :], vcorn.at[3], (up, left)),
+        send(vpr.at[LOW, :], vcorn.at[0], (down, right)),
+        send(vpl.at[LOW, :], vcorn.at[1], (down, left)),
+        send(vpr.at[TOP, :], vcorn.at[2], (up, right)),
+        send(vpl.at[TOP, :], vcorn.at[3], (up, left)),
     ]
     for copy in second:
         copy.wait()
     halos += [
-        send(v.at[:, :, TOP, :], vrows.at[1], (up, j)),
-        send(v.at[:, :, LOW, :], vrows.at[0], (down, j)),
+        send(nat.at[pl.ds(0, 3), :, FIRST, :], vrows.at[1], (up, j)),
+        send(nat.at[pl.ds(0, 3), :, LAST, :], vrows.at[0], (down, j)),
     ]
     y = jnp.dot(s_ext[8 : 8 + n_modes, :], two[...], precision=HIGHEST, preferred_element_type=F32)
     eig = SCREEN + COARSE_SCALE * (row_eig[...] + col_eig[pl.ds(j, 1), :])
@@ -604,7 +646,7 @@
     s_cols, s_ext, t_back, row_eig, col_eig, solution_out, residual_out = refs[:7]
     (
         codes_v, labels_v, right_pack, left_pack, srows, crows, labrows, cols, corners,
-        nat, fxp, fyp, sp, wt, dg, va, vb, sl, v, vpr, vpl,
+        nat, fxp, fyp, sp, wt, dg, va, vb, vpr, vpl,
         lsrc, lfx, lfy, lw, ld, li, lsp, fa, fb, lnat, lnc, lev, lpr, lpl, g,
         one, two, three, mine, spec, back, corr,
         vrows, vcols, vcorn, lrows, lcols, lcorn,
@@ -680,30 +722,33 @@
     fine_operator(nat, fxp, fyp, sp, wt, dg, lfx, lfy, lnat, where)
     level_weights(lfx, lfy, lw, ld, li, lwhere)
 
-    field, other = fine_smooth(va, vb, sp, wt, sl, True)
+    field, other = fine_smooth(va, vb, sp, wt, True)
     for cycle in range(2):
-        fine_residual_to_level(field, sp, wt, dg, sl, lsrc)
+        fine_residual_to_level(field, sp, wt, dg, lsrc)
         level_down(lsrc, li, ld, lw, lsp, fa, fb, lnat, lev, lpr, lpl, g)
-        field_out(field, nat, v, vpr, vpl)
+        field_out(field, nat, vpr, vpl)
         got = [ref.at[cycle] for ref in (vrows, vcols, vcorn, lrows, lcols, lcorn, one, two, three)]
         coarse_solve(
             n_row, n_col, (i, j, up, down, left, right), send, g, s_cols, s_ext, t_back, row_eig, col_eig,
-            v, vpr, vpl, lev, lpr, lpl, *got, mine, spec, back, corr,
+            nat, vpr, vpl, lev, lpr, lpl, *got, mine, spec, back, corr,
         )
         level = level_up(
             lev, got[3], got[4], got[5], corr, lnat, lnc, lfx, lfy, lw, ld, li, lsp, fa, fb, lwhere
         )
-        fine_up(v, got[0], got[1], got[2], level, nat, va, where)
-        field, other = fine_smooth(va, vb, sp, wt, sl, False)
+        fine_up(got[0], got[1], got[2], level, nat, va, where)
+        field, other = fine_smooth(va, vb, sp, wt, False)
         if cycle == 0:
-            field, other = fine_smooth(field, other, sp, wt, sl, False)
-
-    def emit(k, ch, t, here, total):
+            field, other = fine_smooth(field, other, sp, wt, False)
+
+    def emit(k, ch, here, total):
         at = pl.ds(8 + k, 8, stride=K)
-        nat[ch, t, at, :] = here
-        nat[3 + ch, t, at, :] = dg[t, rows8(k), :] * (sp[ch, t, rows8(k), :] - here + total)
-
-    stencil_pass(field, wt, sl, emit, tiles=2)
+        res = [dg[t, rows8(k), :] * (sp[ch, t, rows8(k), :] - here[t] + total[t]) for t in range(3)]
+        for t, x in enumerate(undealt(here, lane)):
+            nat[ch, t, at, :] = x
+        for t, x in enumerate(undealt(res, lane)):
+            nat[3 + ch, t, at, :] = x
+
+    stencil_pass(field, wt, emit, 2)
     stores = []
     for a in range(6):
         for t in range(2):
@@ -734,8 +779,8 @@
         own = slice(CCOLS * j, CCOLS * j + CCOLS)
         s_cols[j, :nc, :CCOLS] = cols[:, own]
         col_eig[j, : 3 * CCOLS] = np.tile(eig(nc)[own], 3)
-        c = LCOLS * j + np.where(lane < 96, lane, lane - 128)
-        ok = (c >= 0) & (c < n_col * LCOLS) & ((lane < 80) | (lane >= 112))
+        c = LCOLS * j + lane - LHALO
+        ok = (c >= 0) & (c < n_col * LCOLS) & (lane < 96)
         t_back[j, :nc, ok] = cols[:, c[ok] // 4].T
     s_ext = np.zeros((nr + 16, nr))
     s_ext[8 : 8 + nr] = rows
@@ -765,8 +810,8 @@
         vmem(2, 2, ROWS, 128), vmem(4, 2, HALO, 128),
         vmem(6, 3, NAT, 128), vmem(3, K * 8, 128), vmem(3, (K + 1) * 8, 128),
         vmem(3, 3, K * 8, 128), vmem(4, 3, K * 8, 128), vmem(3, K * 8, 128),
-        vmem(3, 3, (K + 4) * 8, 128), vmem(3, 3, (K + 4) * 8, 128), vmem(4, 2, 3, 3, 8, 128),
-        vmem(3, 2, ROWS, 128), vmem(1, ROWS, 128), vmem(1, ROWS, 128),
+        vmem(3, 3, (K + 2) * 8, 128), vmem(3, 3, (K + 2) * 8, 128),
+        vmem(ROWS, 128), vmem(ROWS, 128),
         vmem(3, KL * 8, 128), vmem(KL * 8, 128), vmem((KL + 1) * 8, 128),
         vmem(4, KL * 8, 128), vmem(KL * 8, 128), vmem(KL * 8, 128), vmem(3, KL * 8, 128),
         vmem(3, (KL + 2) * 8, 128), vmem(3, (KL + 2) * 8, 128),
@@ -774,7 +819,7 @@
         vmem(LROWS, 128), vmem(LROWS, 128), vmem(CROWS, 128),
         vmem(2, n_col, CROWS, 128), vmem(2, n_row * CROWS, 128), vmem(2, n_col, BROWS, 128),
         vmem(CROWS, 128), vmem(n_row * CROWS, 128), vmem(BROWS, 128), vmem(3, BROWS, 128),
-        vmem(2, 2, 3, 2, HALO, 128), vmem(2, 2, 1, ROWS, 128), vmem(2, 4, 1, HALO, 128),
+        vmem(2, 2, 3, 3, HALO, 128), vmem(2, 2, ROWS, 128), vmem(2, 4, HALO, 128),
         vmem(2, 2, 8, LHALO, 128), vmem(2, 2, LROWS, 128), vmem(2, 4, LHALO, 128),
         pltpu.SemaphoreType.DMA((12,)),
         pltpu.SemaphoreType.DMA((n_copies,)), pltpu.SemaphoreType.DMA((n_copies,)),

time: 208 us -> 179 us (0.86)
  Pallas kernels: 203 us -> 174 us
    pallas_call x1, Pallas kernels: 203 us -> 174 us  [local(): return tuple(call(sources, edge_codes, seam_labels, *consts))]
where the time goes in v3:
time: 179 us
  Pallas kernels  174 us (97%)
  local copies, waits for them, and re-layouts  3.92 us (2%)
    pallas_call x1, Pallas kernels, local(): return tuple(call(sources, edge_codes, seam_labels, *consts))  174 us
    unnamed x4, local copies, waits for them, and re-layouts  3.92 us

profile of v3, /device:TPU:1, one launch (start us, length us, event | category | flops | bytes accessed | tf_op | source)
XLA Modules:
  0.0 178.7 jit_solution(13183466825641162442)
XLA Ops:
  0.6 174.1 %shard_map.95 = (f32[3,512,256]{2,1,0:T(8,128)}, f32[3,512,256]{2,1,0:T(8,128)}) custom-call(f32[3,512,256]{2,1,0:T(8,128)} %src.1, s32[2,512,256]{2,1,0:T(8,128)} %codes.1, s32[512,256]{1,0:T(8,128)} %labels.1, f32[8,128,128]{2,1,0:T(8,128)} %constant.10.clone.refs_0_, f32[528,512]{1,0:T(8,128)} %constant.11.clone.refs_1_, ...), custom_call_target="tpu_custom_call" | custom-call | tf_op jit(solution)/shard_map/pallas_call | solution.py:838
  174.7 0.0 copy-start
  174.7 2.8 %copy.12 = f32[3,512,256]{2,1,0:T(8,128)} copy(f32[3,512,256]{2,1,0:T(8,128)} %get-tuple-element.4) | data formatting | bytes 3145728
  177.5 0.0 copy-done
  177.5 1.1 copy.13
Async XLA Ops:
  174.7 2.8 %copy-start = (f32[3,512,256]{2,1,0:T(8,128)S(1)}, f32[3,512,256]{2,1,0:T(8,128)}, u32[]{:S(2)}) copy-start(f32[3,512,256]{2,1,0:T(8,128)} %get-tuple-element.5) | copy-start | bytes 4718596

commit v4 on v3

--- a/solution.py
+++ b/solution.py
@@ -157,21 +157,25 @@
     lax.fori_loop(0, count, body, 0)
 
 
-def dealt(x, lane):
-    out = []
+def dealt(fields, lane):
+    out = [[] for _ in fields]
     for t in range(3):
         p = 3 * lane + t
-        got = [lanes_take(y, (p - CPAD) % 128) for y in x]
-        out.append(jnp.where((p < 64) | (p >= 320), got[2], jnp.where(p < 192, got[0], got[1])))
+        idx = (p - CPAD) % 128
+        for x, y in zip(fields, out):
+            got = [lanes_take(part, idx) for part in x]
+            y.append(jnp.where((p < 64) | (p >= 320), got[2], jnp.where(p < 192, got[0], got[1])))
     return out
 
 
-def undealt(x, lane):
-    out = []
+def undealt(fields, lane):
+    out = [[] for _ in fields]
     for t in range(2):
         p = lane + (128 * t + CPAD)
-        got = [lanes_take(y, p // 3) for y in x]
-        out.append(jnp.where(p % 3 == 0, got[0], jnp.where(p % 3 == 1, got[1], got[2])))
+        idx = p // 3
+        for x, y in zip(fields, out):
+            got = [lanes_take(part, idx) for part in x]
+            y.append(jnp.where(p % 3 == 0, got[0], jnp.where(p % 3 == 1, got[1], got[2])))
     return out
 
 
@@ -380,6 +384,7 @@
 
     lax.fori_loop(0, LROWS // 8, copy, 0)
     idx = (LHALO + 4 * lane) % 128
+    parts = []
     for i in range(CROWS // 8):
         total = jnp.zeros((8, 128), F32)
         for ch in range(3):
@@ -388,7 +393,10 @@
             x = x + lroll(x, 126)
             x = jnp.where(lane < CCOLS, lanes_take(x, idx), 0.0) * 0.0625
             total = total + lroll(x, CCOLS * ch)
-        g[i * 8 : i * 8 + 8, :] = total
+        parts.append(total)
+    half = len(parts) // 2
+    for i in range(half):
+        g[i * 8 : i * 8 + 8, :] = parts[i] + lroll(parts[half + i], 64)
 
 
 def level_up(lev, lrows, lcols, lcorn, corr, lnat, lnc, fx, fy, lw, ld, li, lsp, fa, fb, where):
@@ -520,10 +528,9 @@
             fx.append(jnp.where((col >= 1) & (col < where[3]), inner, 1.0))
             inner = edge(nat[4, t, above, :], nat[5, t, above, :], label[t])
             fy.append(jnp.where((row >= 1) & (row < where[2]), inner, 1.0))
-        for t, x in enumerate(dealt(fx, lane)):
-            fxp[t, rows8(k), :] = x
-        for t, x in enumerate(dealt(fy, lane)):
-            fyp[t, rows8(k), :] = x
+        for ref, tiles in zip((fxp, fyp), dealt([fx, fy], lane)):
+            for t, x in enumerate(tiles):
+                ref[t, rows8(k), :] = x
         return carry
 
     lax.fori_loop(0, K, faces, 0, unroll=2)
@@ -543,8 +550,9 @@
             dg[t, rows8(k), :] = diag
             for n, face in enumerate((left[t], right[t], up, down)):
                 wt[n, t, rows8(k), :] = face * inv
-        for ch in range(3):
-            for t, x in enumerate(dealt([nat[ch, t, at, :] for t in range(3)], lane)):
+        natural = [[nat[ch, t, at, :] for t in range(3)] for ch in range(3)]
+        for ch, tiles in enumerate(dealt(natural, lane)):
+            for t, x in enumerate(tiles):
                 sp[ch, t, rows8(k), :] = x * scale[t]
         return carry
 
@@ -566,7 +574,7 @@
 
 def coarse_solve(
     n_row, n_col, place, send, g, s_cols, s_ext, t_back, row_eig, col_eig, nat, vpr, vpl, lev, lpr, lpl,
-    vrows, vcols, vcorn, lrows, lcols, lcorn, one, two, three, mine, spec, back, corr,
+    vrows, vcols, vcorn, lrows, lcols, lcorn, one, two, three, mine, full, spec, back, corr,
 ):
     i, j, up, down, left, right = place
     n_modes = n_row * CROWS
@@ -595,7 +603,9 @@
                 x = jnp.zeros((8, 128), F32)
                 for p in range(n_col):
                     here = (lane >= CCOLS * p) & (lane < CCOLS * p + CCOLS)
-                    y = lroll(ref[p, r * 8 : r * 8 + 8, :], CCOLS * (p - ch))
+                    low_half = r * 16 >= n_rows
+                    row = r * 8 - n_rows // 2 if low_half else r * 8
+                    y = lroll(ref[p, row : row + 8, :], CCOLS * (p - ch) - (64 if low_half else 0))
                     x = jnp.where(here, y, x)
                 parts.append(x)
             out.append(jnp.concatenate(parts, axis=0))
@@ -606,10 +616,11 @@
     total = lax.slice_in_dim(x, 0, CROWS)
     for ch in (1, 2):
         total = total + pltpu.roll(lax.slice_in_dim(x, CROWS * ch, CROWS * ch + CROWS), CCOLS * ch, 1)
+    half = CROWS // 2
+    total = lax.slice_in_dim(total, 0, half) + pltpu.roll(lax.slice_in_dim(total, half, CROWS), 64, 1)
     mine[...] = total
-    own = pl.ds(pl.multiple_of(i * CROWS, CROWS), CROWS)
-    second = [send(mine, two.at[own, :], (lax.rem(i + d, n_row), j)) for d in range(1, n_row)]
-    two[own, :] = total
+    second = [send(mine, two.at[i], (lax.rem(i + d, n_row), j)) for d in range(1, n_row)]
+    two[i] = total
     halos += [
         send(vpr, vcols.at[0], (i, right)),
         send(vpl, vcols.at[1], (i, left)),
@@ -624,11 +635,21 @@
         send(nat.at[pl.ds(0, 3), :, FIRST, :], vrows.at[1], (up, j)),
         send(nat.at[pl.ds(0, 3), :, LAST, :], vrows.at[0], (down, j)),
     ]
-    y = jnp.dot(s_ext[8 : 8 + n_modes, :], two[...], precision=HIGHEST, preferred_element_type=F32)
+    for p in range(n_row):
+        for r in range(0, half, 8):
+            x = two[p, r : r + 8, :]
+            full[p * CROWS + r : p * CROWS + r + 8, :] = x
+            full[p * CROWS + half + r : p * CROWS + half + r + 8, :] = lroll(x, 64)
+    y = jnp.dot(s_ext[8 : 8 + n_modes, :], full[...], precision=HIGHEST, preferred_element_type=F32)
     eig = SCREEN + COARSE_SCALE * (row_eig[...] + col_eig[pl.ds(j, 1), :])
     spec[...] = y / eig
     rows = s_ext[pl.ds(pl.multiple_of(i * CROWS, CROWS), BROWS), :]
     z = jnp.dot(rows, spec[...], precision=HIGHEST, preferred_element_type=F32)
+    half = BROWS // 2
+    z = jnp.where(
+        lax.broadcasted_iota(jnp.int32, (half, 128), 1) < 64,
+        lax.slice_in_dim(z, 0, half), pltpu.roll(lax.slice_in_dim(z, half, BROWS), 64, 1),
+    )
     back[...] = z
     third = [send(back, three.at[j], (i, lax.rem(j + d, n_col))) for d in range(1, n_col)]
     three[j] = z
@@ -648,7 +669,7 @@
         codes_v, labels_v, right_pack, left_pack, srows, crows, labrows, cols, corners,
         nat, fxp, fyp, sp, wt, dg, va, vb, vpr, vpl,
         lsrc, lfx, lfy, lw, ld, li, lsp, fa, fb, lnat, lnc, lev, lpr, lpl, g,
-        one, two, three, mine, spec, back, corr,
+        one, two, three, mine, full, spec, back, corr,
         vrows, vcols, vcorn, lrows, lcols, lcorn,
         copy_sems, send_sems, recv_sems,
     ) = refs[7:]
@@ -674,6 +695,13 @@
     for copy in loads:
         copy.start()
     zero_ends(nat, 6)
+    pl.semaphore_wait(barrier, n_col + n_row + 2)
+    send = Sender(send_sems, recv_sems)
+    copies = []
+    for slot, rows, device in ((1, TOP, up), (0, LOW, down)):
+        copies.append(send(src.at[:, rows, :], srows.at[slot], (device, j)))
+        copies.append(send(codes.at[:, rows, :], crows.at[slot], (device, j)))
+        copies.append(send(labels.at[rows, :], labrows.at[slot], (device, j)))
     for copy in loads:
         copy.wait()
 
@@ -693,16 +721,8 @@
         return nat[a, t, pl.ds(pl.multiple_of(8 + PAD + r.start, 8), 8), :]
 
     pack_fine(natural, 6, right_pack, left_pack, lane, ROWS)
-    pl.semaphore_wait(barrier, n_col + n_row + 2)
-    send = Sender(send_sems, recv_sems)
-    copies = [
-        send(right_pack, cols.at[0], (i, right)),
-        send(left_pack, cols.at[1], (i, left)),
-    ]
-    for slot, rows, device in ((1, TOP, up), (0, LOW, down)):
-        copies.append(send(src.at[:, rows, :], srows.at[slot], (device, j)))
-        copies.append(send(codes.at[:, rows, :], crows.at[slot], (device, j)))
-        copies.append(send(labels.at[rows, :], labrows.at[slot], (device, j)))
+    copies.append(send(right_pack, cols.at[0], (i, right)))
+    copies.append(send(left_pack, cols.at[1], (i, left)))
     copies.append(send(right_pack.at[:, LOW, :], corners.at[0], (down, right)))
     copies.append(send(left_pack.at[:, LOW, :], corners.at[1], (down, left)))
     copies.append(send(right_pack.at[:, TOP, :], corners.at[2], (up, right)))
@@ -730,7 +750,7 @@
         got = [ref.at[cycle] for ref in (vrows, vcols, vcorn, lrows, lcols, lcorn, one, two, three)]
         coarse_solve(
             n_row, n_col, (i, j, up, down, left, right), send, g, s_cols, s_ext, t_back, row_eig, col_eig,
-            nat, vpr, vpl, lev, lpr, lpl, *got, mine, spec, back, corr,
+            nat, vpr, vpl, lev, lpr, lpl, *got, mine, full, spec, back, corr,
         )
         level = level_up(
             lev, got[3], got[4], got[5], corr, lnat, lnc, lfx, lfy, lw, ld, li, lsp, fa, fb, lwhere
@@ -740,15 +760,22 @@
         if cycle == 0:
             field, other = fine_smooth(field, other, sp, wt, False)
 
+    fields = []
+
     def emit(k, ch, here, total):
+        fields.append(here)
+        fields.append(
+            [dg[t, rows8(k), :] * (sp[ch, t, rows8(k), :] - here[t] + total[t]) for t in range(3)]
+        )
+
+    def finish(k):
         at = pl.ds(8 + k, 8, stride=K)
-        res = [dg[t, rows8(k), :] * (sp[ch, t, rows8(k), :] - here[t] + total[t]) for t in range(3)]
-        for t, x in enumerate(undealt(here, lane)):
-            nat[ch, t, at, :] = x
-        for t, x in enumerate(undealt(res, lane)):
-            nat[3 + ch, t, at, :] = x
-
-    stencil_pass(field, wt, emit, 2)
+        for n, tiles in enumerate(undealt(fields, lane)):
+            for t, x in enumerate(tiles):
+                nat[n // 2 + 3 * (n % 2), t, at, :] = x
+        fields.clear()
+
+    stencil_pass(field, wt, emit, 1, finish)
     stores = []
     for a in range(6):
         for t in range(2):
@@ -816,9 +843,10 @@
         vmem(4, KL * 8, 128), vmem(KL * 8, 128), vmem(KL * 8, 128), vmem(3, KL * 8, 128),
         vmem(3, (KL + 2) * 8, 128), vmem(3, (KL + 2) * 8, 128),
         vmem(11, LNAT, 128), vmem(3, LNAT, 128), vmem(8, LROWS, 128),
-        vmem(LROWS, 128), vmem(LROWS, 128), vmem(CROWS, 128),
-        vmem(2, n_col, CROWS, 128), vmem(2, n_row * CROWS, 128), vmem(2, n_col, BROWS, 128),
-        vmem(CROWS, 128), vmem(n_row * CROWS, 128), vmem(BROWS, 128), vmem(3, BROWS, 128),
+        vmem(LROWS, 128), vmem(LROWS, 128), vmem(CROWS // 2, 128),
+        vmem(2, n_col, CROWS // 2, 128), vmem(2, n_row, CROWS // 2, 128), vmem(2, n_col, BROWS // 2, 128),
+        vmem(CROWS // 2, 128), vmem(n_row * CROWS, 128), vmem(n_row * CROWS, 128),
+        vmem(BROWS // 2, 128), vmem(3, BROWS, 128),
         vmem(2, 2, 3, 3, HALO, 128), vmem(2, 2, ROWS, 128), vmem(2, 4, HALO, 128),
         vmem(2, 2, 8, LHALO, 128), vmem(2, 2, LROWS, 128), vmem(2, 4, LHALO, 128),
         pltpu.SemaphoreType.DMA((12,)),

time: 179 us -> 177 us (0.989)
  Pallas kernels: 174 us -> 172 us
    pallas_call x1, Pallas kernels: 174 us -> 172 us  [local(): return tuple(call(sources, edge_codes, seam_labels, *consts))]
where the time goes in v4:
time: 177 us
  Pallas kernels  172 us (97%)
  local copies, waits for them, and re-layouts  3.92 us (2%)
    pallas_call x1, Pallas kernels, local(): return tuple(call(sources, edge_codes, seam_labels, *consts))  172 us
    unnamed x4, local copies, waits for them, and re-layouts  3.92 us

profile of v4, /device:TPU:1, one launch (start us, length us, event | category | flops | bytes accessed | tf_op | source)
XLA Modules:
  0.0 176.6 jit_solution(7045384333848417689)
XLA Ops:
  0.6 172.0 %shard_map.95 = (f32[3,512,256]{2,1,0:T(8,128)}, f32[3,512,256]{2,1,0:T(8,128)}) custom-call(f32[3,512,256]{2,1,0:T(8,128)} %src.1, s32[2,512,256]{2,1,0:T(8,128)} %codes.1, s32[512,256]{1,0:T(8,128)} %labels.1, f32[8,128,128]{2,1,0:T(8,128)} %constant.10.clone.refs_0_, f32[528,512]{1,0:T(8,128)} %constant.11.clone.refs_1_, ...), custom_call_target="tpu_custom_call" | custom-call | tf_op jit(solution)/shard_map/pallas_call | solution.py:866
  172.7 0.0 copy-start
  172.7 2.8 %copy.12 = f32[3,512,256]{2,1,0:T(8,128)} copy(f32[3,512,256]{2,1,0:T(8,128)} %get-tuple-element.4) | data formatting | bytes 3145728
  175.5 0.0 copy-done
  175.5 1.1 copy.13
Async XLA Ops:
  172.7 2.8 %copy-start = (f32[3,512,256]{2,1,0:T(8,128)S(1)}, f32[3,512,256]{2,1,0:T(8,128)}, u32[]{:S(2)}) copy-start(f32[3,512,256]{2,1,0:T(8,128)} %get-tuple-element.5) | copy-start | bytes 4718596

commit v5 on v4

--- a/solution.py
+++ b/solution.py
@@ -154,7 +154,7 @@
                 nat[ch, t, dst, :] = x
         return carry
 
-    lax.fori_loop(0, count, body, 0)
+    lax.fori_loop(0, count, body, 0, unroll=2)
 
 
 def dealt(fields, lane):
@@ -399,8 +399,8 @@
         g[i * 8 : i * 8 + 8, :] = parts[i] + lroll(parts[half + i], 64)
 
 
-def level_up(lev, lrows, lcols, lcorn, corr, lnat, lnc, fx, fy, lw, ld, li, lsp, fa, fb, where):
-    lane, sub = lane_iota(), sub_iota()
+def level_halos(lev, lrows, lcols, lcorn, lnat, fx, fy, lw, ld, li, where):
+    lane = lane_iota()
 
     def place(dst_row, count, own, left, right):
         def body(i, carry):
@@ -417,20 +417,23 @@
     place(0, LHALO // 8, lambda a, r: lrows[0, a, r, :], lambda r: lcorn[0, r, :], lambda r: lcorn[1, r, :])
     place(LHALO, LROWS // 8, lambda a, r: lev[a, r, :], lambda r: lcols[0, r, :], lambda r: lcols[1, r, :])
     place(LHALO + LROWS, LHALO // 8, lambda a, r: lrows[1, a, r, :], lambda r: lcorn[2, r, :], lambda r: lcorn[3, r, :])
+    def faces(k, carry):
+        at = pl.ds(LHALO - LPAD + k, 8, stride=KL)
+        fx[rows8(k), :] = lnat[6, at, :]
+        fy[rows8(k), :] = lnat[7, at, :]
+        return carry
+
+    lax.fori_loop(0, KL, faces, 0)
+    level_weights(fx, fy, lw, ld, li, where)
+
+
+def level_up(corr, lnat, lnc, lw, li, lsp, fa, fb, where):
+    lane, sub = lane_iota(), sub_iota()
     for ch in range(3):
         for h in range(LNAT // 32):
             x = corr[ch, 4 + 8 * h : 12 + 8 * h, :]
             for q in range(4):
                 lnc[ch, pl.ds(32 * h + q, 8, stride=4), :] = x
-
-    def faces(k, carry):
-        at = pl.ds(LHALO - LPAD + k, 8, stride=KL)
-        fx[rows8(k), :] = lnat[6, at, :]
-        fy[rows8(k), :] = lnat[7, at, :]
-        return carry
-
-    lax.fori_loop(0, KL, faces, 0)
-    level_weights(fx, fy, lw, ld, li, where)
 
     def fields(k, carry):
         at = pl.ds(LHALO - LPAD + k, 8, stride=KL)
@@ -446,12 +449,15 @@
     return level_smooth(fa, fb, lsp, lw, False)
 
 
-def fine_up(vrows, vcols, vcorn, field, nat, va, where):
-    lane, sub = lane_iota(), sub_iota()
+def fine_halos(vrows, vcols, vcorn, nat):
     unpack_field(nat, 8 + PAD, ROWS // 8, lambda ch, t, i, r: nat[ch, t, r, :], vcols.at[0], vcols.at[1])
     for slot, at in ((0, 8 + PAD - HALO), (1, 8 + PAD + ROWS)):
         own = lambda ch, t, i, r, slot=slot: vrows[slot, ch, t, rows8(i), :]
         unpack_field(nat, at, HALO // 8, own, vcorn.at[2 * slot], vcorn.at[2 * slot + 1])
+
+
+def fine_up(field, nat, va, where):
+    lane, sub = lane_iota(), sub_iota()
 
     def body(kl, carry):
         for t in range(3):
@@ -575,6 +581,7 @@
 def coarse_solve(
     n_row, n_col, place, send, g, s_cols, s_ext, t_back, row_eig, col_eig, nat, vpr, vpl, lev, lpr, lpl,
     vrows, vcols, vcorn, lrows, lcols, lcorn, one, two, three, mine, full, spec, back, corr,
+    field_ready, with_halos,
 ):
     i, j, up, down, left, right = place
     n_modes = n_row * CROWS
@@ -592,6 +599,7 @@
         send(lpr.at[LTOP, :], lcorn.at[2], (up, right)),
         send(lpl.at[LTOP, :], lcorn.at[3], (up, left)),
     ]
+    field_ready()
     for copy in first:
         copy.wait()
 
@@ -612,7 +620,7 @@
         return out
 
     x = jnp.concatenate(placed(one, CROWS), axis=0)
-    x = jnp.dot(x, s_cols[j], precision=HIGHEST, preferred_element_type=F32)
+    x = jnp.dot(x, s_cols[...], precision=HIGHEST, preferred_element_type=F32)
     total = lax.slice_in_dim(x, 0, CROWS)
     for ch in (1, 2):
         total = total + pltpu.roll(lax.slice_in_dim(x, CROWS * ch, CROWS * ch + CROWS), CCOLS * ch, 1)
@@ -653,25 +661,27 @@
     back[...] = z
     third = [send(back, three.at[j], (i, lax.rem(j + d, n_col))) for d in range(1, n_col)]
     three[j] = z
+    for copy in halos:
+        copy.wait()
+    with_halos()
     for copy in third:
         copy.wait()
     z = jnp.concatenate(placed(three, BROWS), axis=0)
-    z = jnp.dot(z, t_back[j], precision=HIGHEST, preferred_element_type=F32)
+    z = jnp.dot(z, t_back[...], precision=HIGHEST, preferred_element_type=F32)
     for ch in range(3):
         corr[ch] = lax.slice_in_dim(z, BROWS * ch, BROWS * ch + BROWS)
-    for copy in halos:
-        copy.wait()
 
 
 def kernel(n_row, n_col, src, codes, labels, *refs):
-    s_cols, s_ext, t_back, row_eig, col_eig, solution_out, residual_out = refs[:7]
+    tables_in, solution_out, residual_out = refs[:5], refs[5], refs[6]
     (
         codes_v, labels_v, right_pack, left_pack, srows, crows, labrows, cols, corners,
         nat, fxp, fyp, sp, wt, dg, va, vb, vpr, vpl,
         lsrc, lfx, lfy, lw, ld, li, lsp, fa, fb, lnat, lnc, lev, lpr, lpl, g,
         one, two, three, mine, full, spec, back, corr,
         vrows, vcols, vcorn, lrows, lcols, lcorn,
-        copy_sems, send_sems, recv_sems,
+        s_cols, s_ext, t_back, row_eig, col_eig,
+        copy_sems, table_sems, send_sems, recv_sems,
     ) = refs[7:]
     i, j = lax.axis_index("row"), lax.axis_index("col")
     up, down = lax.rem(i + n_row - 1, n_row), lax.rem(i + 1, n_row)
@@ -694,6 +704,10 @@
             loads.append(pltpu.make_async_copy(part, nat.at[a, t, MID, :], copy_sems.at[len(loads)]))
     for copy in loads:
         copy.start()
+    table_loads = []
+    for n, (table, ref) in enumerate(zip(tables_in, (s_cols, s_ext, t_back, row_eig, col_eig))):
+        table_loads.append(pltpu.make_async_copy(table.at[j] if n in (0, 2) else table, ref, table_sems.at[n]))
+        table_loads[-1].start()
     zero_ends(nat, 6)
     pl.semaphore_wait(barrier, n_col + n_row + 2)
     send = Sender(send_sems, recv_sems)
@@ -720,9 +734,11 @@
     def natural(a, t, r):
         return nat[a, t, pl.ds(pl.multiple_of(8 + PAD + r.start, 8), 8), :]
 
-    pack_fine(natural, 6, right_pack, left_pack, lane, ROWS)
-    copies.append(send(right_pack, cols.at[0], (i, right)))
-    copies.append(send(left_pack, cols.at[1], (i, left)))
+    for tile, count in ((1, 2), (0, 4)):
+        shifted = lambda a, t, r, tile=tile: natural(4 * tile + a, t, r)
+        pack_fine(shifted, count, right_pack.at[pl.ds(tile, 1)], left_pack.at[pl.ds(tile, 1)], lane, ROWS)
+        copies.append(send(right_pack.at[tile], cols.at[0, tile], (i, right)))
+        copies.append(send(left_pack.at[tile], cols.at[1, tile], (i, left)))
     copies.append(send(right_pack.at[:, LOW, :], corners.at[0], (down, right)))
     copies.append(send(left_pack.at[:, LOW, :], corners.at[1], (down, left)))
     copies.append(send(right_pack.at[:, TOP, :], corners.at[2], (up, right)))
@@ -746,16 +762,24 @@
     for cycle in range(2):
         fine_residual_to_level(field, sp, wt, dg, lsrc)
         level_down(lsrc, li, ld, lw, lsp, fa, fb, lnat, lev, lpr, lpl, g)
-        field_out(field, nat, vpr, vpl)
         got = [ref.at[cycle] for ref in (vrows, vcols, vcorn, lrows, lcols, lcorn, one, two, three)]
+
+        def field_ready(field=field, cycle=cycle):
+            field_out(field, nat, vpr, vpl)
+            if cycle == 0:
+                for copy in table_loads:
+                    copy.wait()
+
+        def with_halos(got=got):
+            level_halos(lev, got[3], got[4], got[5], lnat, lfx, lfy, lw, ld, li, lwhere)
+            fine_halos(got[0], got[1], got[2], nat)
+
         coarse_solve(
             n_row, n_col, (i, j, up, down, left, right), send, g, s_cols, s_ext, t_back, row_eig, col_eig,
-            nat, vpr, vpl, lev, lpr, lpl, *got, mine, full, spec, back, corr,
+            nat, vpr, vpl, lev, lpr, lpl, *got, mine, full, spec, back, corr, field_ready, with_halos,
         )
-        level = level_up(
-            lev, got[3], got[4], got[5], corr, lnat, lnc, lfx, lfy, lw, ld, li, lsp, fa, fb, lwhere
-        )
-        fine_up(got[0], got[1], got[2], level, nat, va, where)
+        level = level_up(corr, lnat, lnc, lw, li, lsp, fa, fb, lwhere)
+        fine_up(level, nat, va, where)
         field, other = fine_smooth(va, vb, sp, wt, False)
         if cycle == 0:
             field, other = fine_smooth(field, other, sp, wt, False)
@@ -829,7 +853,7 @@
     def vmem(*dims, dtype=F32):
         return pltpu.VMEM(dims, dtype)
 
-    n_copies = 12 + 2 * (2 * (n_col - 1) + (n_row - 1) + 16)
+    n_copies = 14 + 2 * (2 * (n_col - 1) + (n_row - 1) + 16)
     scratch = [
         vmem(2, ROWS, COLS, dtype=jnp.int32), vmem(ROWS, COLS, dtype=jnp.int32),
         vmem(2, ROWS, 128), vmem(2, ROWS, 128),
@@ -849,13 +873,15 @@
         vmem(BROWS // 2, 128), vmem(3, BROWS, 128),
         vmem(2, 2, 3, 3, HALO, 128), vmem(2, 2, ROWS, 128), vmem(2, 4, HALO, 128),
         vmem(2, 2, 8, LHALO, 128), vmem(2, 2, LROWS, 128), vmem(2, 4, LHALO, 128),
-        pltpu.SemaphoreType.DMA((12,)),
+        vmem(128, 128), vmem(n_row * CROWS + 16, n_row * CROWS), vmem(128, 128),
+        vmem(n_row * CROWS, 128), vmem(n_col, 128),
+        pltpu.SemaphoreType.DMA((12,)), pltpu.SemaphoreType.DMA((5,)),
         pltpu.SemaphoreType.DMA((n_copies,)), pltpu.SemaphoreType.DMA((n_copies,)),
     ]
     call = pl.pallas_call(
         functools.partial(kernel, n_row, n_col),
         out_shape=[shape(3, ROWS, COLS)] * 2,
-        in_specs=[IN_ANY] * 3 + [IN_VMEM] * 5,
+        in_specs=[IN_ANY] * 8,
         out_specs=[IN_ANY] * 2,
         scratch_shapes=scratch,
         compiler_params=pltpu.CompilerParams(collective_id=0, has_side_effects=True, vmem_limit_bytes=VMEM_LIMIT),

time: 177 us -> 164 us (0.927)
  Pallas kernels: 172 us -> 159 us
    pallas_call x1, Pallas kernels: 172 us -> 159 us  [local(): return tuple(call(sources, edge_codes, seam_labels, *consts))]
where the time goes in v5:
time: 164 us
  Pallas kernels  159 us (97%)
  local copies, waits for them, and re-layouts  3.92 us (2%)
    pallas_call x1, Pallas kernels, local(): return tuple(call(sources, edge_codes, seam_labels, *consts))  159 us
    unnamed x4, local copies, waits for them, and re-layouts  3.92 us

profile of v5, /device:TPU:1, one launch (start us, length us, event | category | flops | bytes accessed | tf_op | source)
XLA Modules:
  0.0 163.9 jit_solution(15251978862360053158)
XLA Ops:
  0.6 159.4 %shard_map.95 = (f32[3,512,256]{2,1,0:T(8,128)}, f32[3,512,256]{2,1,0:T(8,128)}) custom-call(f32[3,512,256]{2,1,0:T(8,128)} %src.1, s32[2,512,256]{2,1,0:T(8,128)} %codes.1, s32[512,256]{1,0:T(8,128)} %labels.1, f32[8,128,128]{2,1,0:T(8,128)} %constant.10.clone.refs_0_, f32[528,512]{1,0:T(8,128)} %constant.11.clone.refs_1_, ...), custom_call_target="tpu_custom_call" | custom-call | tf_op jit(solution)/shard_map/pallas_call | solution.py:892
  160.0 0.0 copy-start
  160.0 2.8 %copy.12 = f32[3,512,256]{2,1,0:T(8,128)} copy(f32[3,512,256]{2,1,0:T(8,128)} %get-tuple-element.4) | data formatting | bytes 3145728
  162.8 0.0 copy-done
  162.8 1.1 copy.13
Async XLA Ops:
  160.0 2.8 %copy-start = (f32[3,512,256]{2,1,0:T(8,128)S(1)}, f32[3,512,256]{2,1,0:T(8,128)}, u32[]{:S(2)}) copy-start(f32[3,512,256]{2,1,0:T(8,128)} %get-tuple-element.5) | copy-start | bytes 4718596

commit v6 on v5

--- a/solution.py
+++ b/solution.py
@@ -166,6 +166,23 @@
             got = [lanes_take(part, idx) for part in x]
             y.append(jnp.where((p < 64) | (p >= 320), got[2], jnp.where(p < 192, got[0], got[1])))
     return out
+
+
+def deal_sources(nat, out, at, count, parts):
+    lane = lane_iota()
+
+    def body(i, carry):
+        r = pl.ds(pl.multiple_of(at + 8 * i, 8), 8)
+        for t in range(3):
+            p = 3 * lane + t
+            idx = (p - CPAD) % 128
+            for ch in range(3):
+                got = {n: lanes_take(nat[ch, n, r, :], idx) for n in parts}
+                x = jnp.where(p < 192, got[0], got[1]) if 0 in got else out[ch, t, r, :]
+                out[ch, t, r, :] = jnp.where((p < 64) | (p >= 320), got[2], x) if 2 in got else x
+        return carry
+
+    lax.fori_loop(0, count, body, 0, unroll=2)
 
 
 def undealt(fields, lane):
@@ -516,7 +533,7 @@
         return copy
 
 
-def fine_operator(nat, fxp, fyp, sp, wt, dg, lfx, lfy, lnat, where):
+def fine_operator(nat, dealt_src, fxp, fyp, sp, wt, dg, lfx, lfy, lnat, where):
     lane, sub = lane_iota(), sub_iota()
 
     def edge(code, a, b):
@@ -556,10 +573,9 @@
             dg[t, rows8(k), :] = diag
             for n, face in enumerate((left[t], right[t], up, down)):
                 wt[n, t, rows8(k), :] = face * inv
-        natural = [[nat[ch, t, at, :] for t in range(3)] for ch in range(3)]
-        for ch, tiles in enumerate(dealt(natural, lane)):
-            for t, x in enumerate(tiles):
-                sp[ch, t, rows8(k), :] = x * scale[t]
+        for ch in range(3):
+            for t in range(3):
+                sp[ch, t, rows8(k), :] = dealt_src[ch, t, at, :] * scale[t]
         return carry
 
     lax.fori_loop(0, K, weights, 0, unroll=2)
@@ -743,6 +759,12 @@
     copies.append(send(left_pack.at[:, LOW, :], corners.at[1], (down, left)))
     copies.append(send(right_pack.at[:, TOP, :], corners.at[2], (up, right)))
     copies.append(send(left_pack.at[:, TOP, :], corners.at[3], (up, left)))
+    zero = jnp.zeros((8, 128), F32)
+    for ch in range(3):
+        for t in range(3):
+            for r in (0, 8, 16, NAT - 24, NAT - 16, NAT - 8):
+                va[ch, t, r : r + 8, :] = zero
+    deal_sources(nat, va, 8 + PAD, ROWS // 8, (0, 1))
     for copy in copies:
         copy.wait()
 
@@ -755,7 +777,10 @@
                 nat[3 + a, t, rows, :] = crows[slot, a, :, c].astype(F32)
             nat[5, t, rows, :] = labrows[slot, :, c].astype(F32)
     unpack_columns(nat, 6, cols, corners, lane)
-    fine_operator(nat, fxp, fyp, sp, wt, dg, lfx, lfy, lnat, where)
+    deal_sources(nat, va, 8 + PAD - HALO, HALO // 8, (0, 1, 2))
+    deal_sources(nat, va, 8 + PAD, ROWS // 8, (2,))
+    deal_sources(nat, va, 8 + PAD + ROWS, HALO // 8, (0, 1, 2))
+    fine_operator(nat, va, fxp, fyp, sp, wt, dg, lfx, lfy, lnat, where)
     level_weights(lfx, lfy, lw, ld, li, lwhere)
 
     field, other = fine_smooth(va, vb, sp, wt, True)
@@ -784,29 +809,41 @@
         if cycle == 0:
             field, other = fine_smooth(field, other, sp, wt, False)
 
+    def solution_rows(m, carry):
+        ks = (2 * m, 2 * m + 1)
+        fields = [[field[ch, t, rows8(k + 1), :] for t in range(3)] for k in ks for ch in range(3)]
+        for n, tiles in enumerate(undealt(fields, lane)):
+            for t, x in enumerate(tiles):
+                nat[n % 3, t, pl.ds(8 + ks[n // 3], 8, stride=K), :] = x
+        return carry
+
+    lax.fori_loop(0, K // 2, solution_rows, 0)
+    stores = []
+
+    def store(first, ref):
+        for a in range(3):
+            for t in range(2):
+                out = ref.at[a, :, pl.ds(128 * t, 128)]
+                copy = pltpu.make_async_copy(nat.at[first + a, t, MID, :], out, copy_sems.at[len(stores)])
+                copy.start()
+                stores.append(copy)
+
+    store(0, solution_out)
     fields = []
 
     def emit(k, ch, here, total):
-        fields.append(here)
         fields.append(
             [dg[t, rows8(k), :] * (sp[ch, t, rows8(k), :] - here[t] + total[t]) for t in range(3)]
         )
 
-    def finish(k):
-        at = pl.ds(8 + k, 8, stride=K)
+    def finish(m):
         for n, tiles in enumerate(undealt(fields, lane)):
             for t, x in enumerate(tiles):
-                nat[n // 2 + 3 * (n % 2), t, at, :] = x
+                nat[3 + n % 3, t, pl.ds(8 + 2 * m + n // 3, 8, stride=K), :] = x
         fields.clear()
 
-    stencil_pass(field, wt, emit, 1, finish)
-    stores = []
-    for a in range(6):
-        for t in range(2):
-            out = (solution_out if a < 3 else residual_out).at[a % 3, :, pl.ds(128 * t, 128)]
-            stores.append(pltpu.make_async_copy(nat.at[a, t, MID, :], out, copy_sems.at[len(stores)]))
-    for copy in stores:
-        copy.start()
+    stencil_pass(field, wt, emit, 2, finish)
+    store(3, residual_out)
     for copy in stores:
         copy.wait()
 

time: 164 us -> 163 us (level)
  no operation moved by 1% of the time
where the time goes in v6:
time: 163 us
  Pallas kernels  158 us (97%)
  local copies, waits for them, and re-layouts  3.92 us (2%)
    pallas_call x1, Pallas kernels, local(): return tuple(call(sources, edge_codes, seam_labels, *consts))  158 us
    unnamed x4, local copies, waits for them, and re-layouts  3.92 us

profile of v6, /device:TPU:1, one launch (start us, length us, event | category | flops | bytes accessed | tf_op | source)
XLA Modules:
  0.0 162.5 jit_solution(14095500159247367845)
XLA Ops:
  0.6 158.0 %shard_map.95 = (f32[3,512,256]{2,1,0:T(8,128)}, f32[3,512,256]{2,1,0:T(8,128)}) custom-call(f32[3,512,256]{2,1,0:T(8,128)} %src.1, s32[2,512,256]{2,1,0:T(8,128)} %codes.1, s32[512,256]{1,0:T(8,128)} %labels.1, f32[8,128,128]{2,1,0:T(8,128)} %constant.10.clone.refs_0_, f32[528,512]{1,0:T(8,128)} %constant.11.clone.refs_1_, ...), custom_call_target="tpu_custom_call" | custom-call | tf_op jit(solution)/shard_map/pallas_call | solution.py:929
  158.6 0.0 copy-start
  158.6 2.8 %copy.12 = f32[3,512,256]{2,1,0:T(8,128)} copy(f32[3,512,256]{2,1,0:T(8,128)} %get-tuple-element.4) | data formatting | bytes 3145728
  161.4 0.0 copy-done
  161.4 1.1 copy.13
Async XLA Ops:
  158.6 2.8 %copy-start = (f32[3,512,256]{2,1,0:T(8,128)S(1)}, f32[3,512,256]{2,1,0:T(8,128)}, u32[]{:S(2)}) copy-start(f32[3,512,256]{2,1,0:T(8,128)} %get-tuple-element.5) | copy-start | bytes 4718596

commit v7 on v6

--- a/solution.py
+++ b/solution.py
@@ -653,12 +653,12 @@
         send(vpr.at[TOP, :], vcorn.at[2], (up, right)),
         send(vpl.at[TOP, :], vcorn.at[3], (up, left)),
     ]
-    for copy in second:
-        copy.wait()
     halos += [
         send(nat.at[pl.ds(0, 3), :, FIRST, :], vrows.at[1], (up, j)),
         send(nat.at[pl.ds(0, 3), :, LAST, :], vrows.at[0], (down, j)),
     ]
+    for copy in second:
+        copy.wait()
     for p in range(n_row):
         for r in range(0, half, 8):
             x = two[p, r : r + 8, :]

time: 163 us -> 159 us (0.975)
  Pallas kernels: 158 us -> 154 us
    pallas_call x1, Pallas kernels: 158 us -> 154 us  [local(): return tuple(call(sources, edge_codes, seam_labels, *consts))]
where the time goes in v7:
time: 159 us
  Pallas kernels  154 us (97%)
  local copies, waits for them, and re-layouts  3.92 us (2%)
    pallas_call x1, Pallas kernels, local(): return tuple(call(sources, edge_codes, seam_labels, *consts))  154 us
    unnamed x4, local copies, waits for them, and re-layouts  3.92 us

profile of v7, /device:TPU:1, one launch (start us, length us, event | category | flops | bytes accessed | tf_op | source)
XLA Modules:
  0.0 158.5 jit_solution(1453988082572609192)
XLA Ops:
  0.6 154.0 %shard_map.95 = (f32[3,512,256]{2,1,0:T(8,128)}, f32[3,512,256]{2,1,0:T(8,128)}) custom-call(f32[3,512,256]{2,1,0:T(8,128)} %src.1, s32[2,512,256]{2,1,0:T(8,128)} %codes.1, s32[512,256]{1,0:T(8,128)} %labels.1, f32[8,128,128]{2,1,0:T(8,128)} %constant.10.clone.refs_0_, f32[528,512]{1,0:T(8,128)} %constant.11.clone.refs_1_, ...), custom_call_target="tpu_custom_call" | custom-call | tf_op jit(solution)/shard_map/pallas_call | solution.py:929
  154.6 0.0 copy-start
  154.6 2.8 %copy.12 = f32[3,512,256]{2,1,0:T(8,128)} copy(f32[3,512,256]{2,1,0:T(8,128)} %get-tuple-element.4) | data formatting | bytes 3145728
  157.4 0.0 copy-done
  157.4 1.1 copy.13
Async XLA Ops:
  154.6 2.8 %copy-start = (f32[3,512,256]{2,1,0:T(8,128)S(1)}, f32[3,512,256]{2,1,0:T(8,128)}, u32[]{:S(2)}) copy-start(f32[3,512,256]{2,1,0:T(8,128)} %get-tuple-element.5) | copy-start | bytes 4718596
